TPU v7x, 32 devices: a whole 2x2x4 slice. The times are simulated.
32 devices in a mesh: seq: 4 (over z), phase: 4 (over y, x), dp: 2 (over core).
Axes of the slice: x: 2, y: 2, z: 4, core: 2. Of those that a mesh axis runs over, the one named last changes fastest.
Arguments:
- byte_embed: bfloat16 [4096, 1536], P(('dp', 'seq')), parts along dimension 0, may hold values from -6 to 6
- in_gain: float32 [1536], replicated, may hold values from 0.25 to 1.75
- w_qkv: bfloat16 [1536, 3, 1536], P('seq', None, 'phase')
- w_up: bfloat16 [1536, 3072], P('phase')
- out_gain: float32 [3072], P('phase'), may hold values from 0.25 to 1.75
- bounds: int32 [1024], P(('dp', 'seq')), parts along dimension 0, may hold values from 0 to 2047, as said below
- owner: int32 [1024, 1], P(('dp', 'seq')), parts along dimension 0, may hold values from 0 to 3; in each aligned block of 128 rows (0 to 127, 128 to 255, ...) at most 64 rows name the same one
Outputs:
- byte_states: bfloat16 [4096, 1536], P(('dp', 'seq'), 'phase'), parts along dimension 0
- stretch_states: bfloat16 [2048, 3072], P(('dp', 'seq'), 'phase'), parts along dimension 0
There are 2 independent parts, one for each index of `dp`. A program takes and returns all parts, laid end to end along the dimension named above; an argument that names none is the same for every part. Nothing has to cross between parts.
Inputs may be any that keep to these rules, and one draw needn't show every extreme that they name: `bounds`: strictly rising; the 128 entries of block b lie in bytes b * 512 to (b + 1) * 512 - 1, and the first and last byte of each block are among them. Among the 128 stretch rows of one block no owner is named more than 64 times.
All inputs are finite; a program needn't handle non-finite values.
Results may differ from a plain program's by a relative error of at most 0.013.
Values may be sent and summed in bfloat16 or wider, within the bound.
A program may use at most 128 MiB of HBM per device.

v0:
```python
import functools
import math
import jax
import jax.numpy as jnp
from jax import lax
from jax.experimental import pallas as pl
from jax.experimental.pallas import tpu as pltpu
from jax.sharding import PartitionSpec as P

DC = 3072
HD = 128
WINDOW = 1024
MESH = pl.DeviceIdType.MESH
NEG = -0.7 * 3.4e38


def fused_kernel(
    dims,
    x_ref,
    gain_ref,
    w_ref,
    up_ref,
    og_ref,
    bounds_ref,
    owner_ref,
    bs_ref,
    ss_ref,
    xbuf,
    normed,
    halo,
    wbuf,
    upbuf,
    qbuf,
    kbuf,
    vbuf,
    obuf,
    mbuf,
    lbuf,
    rowbuf,
    sqbuf,
    outbuf,
    loc_sem,
    w_send,
    w_recv,
    p_send,
    p_recv,
    up_send,
    up_recv,
    upp_send,
    upp_recv,
    h_send,
    h_recv,
    g_send,
    g_recv,
    row_send,
    row_recv,
    sq_send,
    sq_recv,
    a_send,
    a_recv,
):
    n_seq, n_phase, reach, slot = dims
    tok, d = xbuf.shape
    rows, width = w_ref.shape[1:]
    half = rows // 2
    heads = width // HD
    crows = bounds_ref.shape[1]
    cols = og_ref.shape[1]
    z = lax.axis_index("seq")
    p = lax.axis_index("phase")
    c = lax.axis_index("dp")

    own_x = pltpu.make_async_copy(x_ref, xbuf, loc_sem.at[0])
    own_x.start()
    own_up = pltpu.make_async_copy(
        up_ref.at[:, pl.ds(pl.multiple_of(p * cols, 128), cols)], upbuf.at[p], loc_sem.at[1]
    )
    own_up.start()
    own_w = []
    for h in range(heads):
        own_w.append(
            pltpu.make_async_copy(
                w_ref.at[:, :, pl.ds(h * HD, HD)],
                wbuf.at[h, :, pl.ds(pl.multiple_of(z * rows, rows), rows), :],
                loc_sem.at[2 + h],
            )
        )
        own_w[h].start()

    twin_core = {"dp": 1 - c}
    peers = (
        [{"seq": lax.rem(z + k, n_seq)} for k in range(1, n_seq)]
        + [{"phase": lax.rem(p + k, n_phase)} for k in range(1, n_phase)]
        + [twin_core]
    )
    barrier = pltpu.get_barrier_semaphore()
    for peer in peers:
        pl.semaphore_signal(barrier, inc=1, device_id=peer, device_id_type=MESH)
    pl.semaphore_wait(barrier, len(peers))

    pending = []

    def when(cond, action):
        if cond is None:
            action()
        else:
            pl.when(cond)(action)

    def send(src, dst, ssem, rsem, peer, cond=None):
        copy = pltpu.make_async_remote_copy(
            src_ref=src, dst_ref=dst, send_sem=ssem, recv_sem=rsem, device_id=peer, device_id_type=MESH
        )
        when(cond, copy.start)
        pending.append((cond, copy))
        return copy

    right, left = {"seq": z + 1}, {"seq": z - 1}
    has_right, has_left = z < n_seq - 1, z > 0
    ways = ((right, has_right, -1), (left, has_left, 1))

    def chunk(h, shard):
        at = pl.multiple_of(shard * rows + c * half, half)
        return wbuf.at[h, :, pl.ds(at, half), :]

    def issue_own(h):
        if h >= heads or h in issued:
            return
        issued.add(h)
        src = w_ref.at[:, pl.ds(pl.multiple_of(c * half, half), half), pl.ds(h * HD, HD)]
        for way, (peer, cond, sign) in enumerate(ways):
            send(src, chunk(h, z), w_send.at[way, h, 0], w_recv.at[way, h, 0], peer, cond)

    twins = {}
    issued = set()
    LEFTWARD, RIGHTWARD = 1, 0

    def relay(h, t, *which):
        for way in which:
            if h >= heads or t >= n_seq or (h, t, way) in twins:
                continue
            peer, cond, sign = ways[way]
            shard = z + sign * t
            there = (shard >= 0) & (shard < n_seq)
            piece = chunk(h, jnp.clip(shard, 0, n_seq - 1))
            got = pltpu.make_async_remote_copy(
                src_ref=piece,
                dst_ref=piece,
                send_sem=w_send.at[way, h, t - 1],
                recv_sem=w_recv.at[way, h, t - 1],
                device_id=peer,
                device_id_type=MESH,
            )
            pl.when(there)(got.wait_recv)
            if t < n_seq - 1:
                send(piece, piece, w_send.at[way, h, t], w_recv.at[way, h, t], peer, there & cond)
            twins[h, t, way] = (
                there,
                send(piece, piece, p_send.at[way, h, t - 1], p_recv.at[way, h, t - 1], twin_core, there),
            )

    def finish(h):
        own_w[h].wait()
        for t in range(1, n_seq):
            relay(h, t, LEFTWARD, RIGHTWARD)
        for t in range(1, n_seq):
            for way in range(2):
                there, twin = twins[h, t, way]
                pl.when(there)(twin.wait_recv)

    across = {1: {"phase": p + 1 - 2 * lax.rem(p, 2)}, 2: {"phase": lax.rem(p + 2, n_phase)}}
    spots = {k: v["phase"] for k, v in across.items()}
    mine = {}

    def halo_start(dist, cond):
        own = normed.at[:, pl.ds(pl.multiple_of(p * width, 128), width)]
        src = own if dist == 1 else halo.at[dist - 2, p]
        mine[dist] = send(src, halo.at[dist - 1, p], h_send.at[dist - 1], h_recv.at[dist - 1], right, cond)

    gathers = {}

    def halo_spread(dist):
        there = z >= dist
        pl.when(there)(mine[dist].wait_recv)
        if dist < reach:
            halo_start(dist + 1, there & has_right)
        for k in (1, 2):
            piece = halo.at[dist - 1, p]
            gathers[dist, k] = send(
                piece, piece, g_send.at[dist - 1, k - 1], g_recv.at[dist - 1, k - 1], across[k], there
            )

    def halo_pass(dist):
        there = z >= dist
        for k in (1, 2):
            pl.when(there)(gathers[dist, k].wait_recv)
            part = pl.ds((k - 1) * (tok // 2), tok // 2)
            piece = halo.at[dist - 1, spots[k], part]
            gathers[dist, 2 + k] = send(
                piece, piece, g_send.at[dist - 1, k + 1], g_recv.at[dist - 1, k + 1], across[3 - k], there
            )

    def halo_wait(dist):
        @pl.when(z >= dist)
        def _():
            for k in (1, 2):
                gathers[dist, 2 + k].wait_recv()

    issue_own(0)
    up_rows = up_ref.shape[0] // 2
    up_half = pl.ds(pl.multiple_of(c * up_rows, up_rows), up_rows)
    up_copies, up_twins = [], []
    for k in range(1, n_phase):
        other = lax.rem(p + k, n_phase)
        part = pl.ds(pl.multiple_of(other * cols, 128), cols)
        up_copies.append(
            send(
                up_ref.at[up_half, part],
                upbuf.at[p, up_half],
                up_send.at[k - 1],
                up_recv.at[k - 1],
                {"phase": other},
            )
        )

    own_x.wait()
    step_rows = 64

    @pl.loop(0, tok // step_rows)
    def _(i):
        r = pl.ds(pl.multiple_of(i * step_rows, step_rows), step_rows)
        xx = xbuf[r, :].astype(jnp.float32)
        scale = lax.rsqrt(jnp.mean(xx * xx, axis=1, keepdims=True) + 1e-05)
        normed[r, :] = (xx * scale * gain_ref[...]).astype(jnp.bfloat16)

    relay(0, 1, LEFTWARD)
    halo_start(1, has_right)

    def column(ref):
        wide = jnp.broadcast_to(ref[...].astype(jnp.float32), (crows, crows))
        return wide.T

    local = column(bounds_ref)[:, 0:1] - (z * tok).astype(jnp.float32)
    spot = lax.broadcasted_iota(jnp.int32, (crows, tok), 1).astype(jnp.float32)
    pick = jnp.where(local == spot, 1.0, 0.0).astype(jnp.bfloat16)
    same = column(owner_ref) == owner_ref[...].astype(jnp.float32)
    before = lax.broadcasted_iota(jnp.int32, (crows, crows), 0) < lax.broadcasted_iota(
        jnp.int32, (crows, crows), 1
    )
    rank = jnp.sum(jnp.where(same & before, 1, 0), axis=0, keepdims=True)
    target = owner_ref[...] * slot + rank
    place = jnp.where(
        target == lax.broadcasted_iota(jnp.int32, (n_seq * slot, crows), 0), 1.0, 0.0
    ).astype(jnp.bfloat16)

    tq = min(tok, 256)
    scale = HD ** (-0.5) * math.log2(math.e)

    def attend(dist, h):
        for q0 in range(0, tok, tq):
            r = pl.ds(q0, tq)
            low = max(0, q0 + dist * tok - WINDOW + 1) // 128 * 128
            keys = slice(low, tok if dist else q0 + tq)
            s = lax.dot_general(
                qbuf[h, r, :],
                kbuf[dist, keys],
                (((1,), (1,)), ((), ())),
                preferred_element_type=jnp.float32,
            )
            if dist == 0 or (dist + 1) * tok - 1 >= WINDOW:
                qi = q0 + lax.broadcasted_iota(jnp.int32, s.shape, 0)
                kj = lax.broadcasted_iota(jnp.int32, s.shape, 1) + (low - dist * tok)
                s = jnp.where((kj <= qi) & (kj > qi - WINDOW), s, NEG)
            top = jnp.max(s, axis=1, keepdims=True)
            if dist > 0:
                old = mbuf[h, r, :]
                top = jnp.maximum(top, old)
            e = jnp.exp2(s * scale - top * scale)
            total = jnp.sum(e, axis=1, keepdims=True)
            o = jnp.dot(e.astype(jnp.bfloat16), vbuf[dist, keys], preferred_element_type=jnp.float32)
            if dist > 0:
                fade = jnp.exp2((old - top) * scale)
                total = total + fade * lbuf[h, r, :]
                o = o + fade * obuf[h, r, :]
            mbuf[h, r, :] = top
            lbuf[h, r, :] = total
            obuf[h, r, :] = o

    def own_block(h):
        w = jnp.concatenate([wbuf[h, j] for j in range(3)], axis=1)
        got = jnp.dot(normed[...], w, preferred_element_type=jnp.float32).astype(jnp.bfloat16)
        qbuf[h] = got[:, :HD]
        kbuf[0] = got[:, HD : 2 * HD]
        vbuf[0] = got[:, 2 * HD :]
        attend(0, h)

    def earlier_block(h, dist):
        @pl.when(z >= dist)
        def _():
            w = jnp.concatenate([wbuf[h, j] for j in range(1, 3)], axis=1)
            rows_in = jnp.concatenate([halo[dist - 1, q] for q in range(n_phase)], axis=1)
            got = jnp.dot(rows_in, w, preferred_element_type=jnp.float32).astype(jnp.bfloat16)
            kbuf[dist] = got[:, :HD]
            vbuf[dist] = got[:, HD:]
            attend(dist, h)

    row_copies = []

    def close(h):
        at = slice(h * HD, (h + 1) * HD)
        res = xbuf[:, pl.ds(pl.multiple_of(p * width + h * HD, HD), HD)].astype(jnp.float32)
        att = (obuf[h] / lbuf[h]).astype(jnp.bfloat16).astype(jnp.float32)
        states = (res + att).astype(jnp.bfloat16)
        bs_ref[:, at] = states
        rowbuf[h, p] = jnp.dot(pick, states, preferred_element_type=jnp.float32).astype(jnp.bfloat16)
        for k in range(1, n_phase):
            row_copies.append(
                send(
                    rowbuf.at[h, p],
                    rowbuf.at[h, p],
                    row_send.at[h, k - 1],
                    row_recv.at[h, k - 1],
                    {"phase": lax.rem(p + k, n_phase)},
                )
            )

    halo_spread(1)
    issue_own(1)
    relay(0, 1, RIGHTWARD)
    for t in range(2, n_seq):
        relay(0, t, LEFTWARD)
    for dist in range(2, reach + 1):
        halo_spread(dist)
        halo_pass(dist - 1)
    relay(1, 1, LEFTWARD, RIGHTWARD)
    issue_own(2)
    relay(0, 2, RIGHTWARD)
    for k in range(1, n_phase):
        up_copies[k - 1].wait_recv()
        piece = upbuf.at[lax.rem(p + n_phase - k, n_phase), up_half]
        up_twins.append(send(piece, piece, upp_send.at[k - 1], upp_recv.at[k - 1], twin_core))
    for t in range(2, n_seq):
        relay(1, t, LEFTWARD)

    for h in range(heads):
        issue_own(h + 1)
        finish(h)
        own_block(h)
        relay(h + 2, 1, LEFTWARD, RIGHTWARD)
        if h == 0:
            halo_pass(reach)
        relay(h + 1, 2, LEFTWARD, RIGHTWARD)
        for dist in range(1, reach):
            if h == 0:
                halo_wait(dist)
            earlier_block(h, dist)
        relay(h + 2, 2, LEFTWARD, RIGHTWARD)
        issue_own(h + 3)
    halo_wait(reach)
    for h in range(heads):
        earlier_block(h, reach)
        close(h)

    own_up.wait()
    for twin in up_twins:
        twin.wait_recv()

    def piece(s):
        got = jnp.dot(
            jnp.concatenate([rowbuf[h, s] for h in range(heads)], axis=1),
            upbuf[s],
            preferred_element_type=jnp.float32,
        )
        return got.astype(jnp.bfloat16).astype(jnp.float32)

    projected = piece(p)
    for copy in row_copies:
        copy.wait_recv()
    for k in range(1, n_phase):
        projected = projected + piece(lax.rem(p + k, n_phase))
    sq = jnp.sum(projected * projected, axis=1, keepdims=True)
    sqbuf[p] = jnp.broadcast_to(sq, (crows, crows)).T[0:8, :]
    sq_copies = []
    for k in range(1, n_phase):
        other = lax.rem(p + k, n_phase)
        sq_copies.append(
            send(sqbuf.at[p], sqbuf.at[p], sq_send.at[k - 1], sq_recv.at[k - 1], {"phase": other})
        )
    for copy in sq_copies:
        copy.wait_recv()
    all_sq = sqbuf[0]
    for k in range(1, n_phase):
        all_sq = all_sq + sqbuf[k]
    all_sq = jnp.broadcast_to(all_sq[0:1, :], (crows, crows)).T[:, 0:1]
    norm = lax.rsqrt(all_sq / (n_phase * cols) + 1e-05)
    main_in = (projected * norm * og_ref[...]).astype(jnp.bfloat16)
    routed = jnp.dot(place, main_in, preferred_element_type=jnp.float32).astype(jnp.bfloat16)
    for s in range(n_seq):
        outbuf[s] = routed[s * slot : (s + 1) * slot]
    a_copies = []
    for k in range(1, n_seq):
        other = lax.rem(z + k, n_seq)
        a_copies.append(
            send(outbuf.at[other], ss_ref.at[z], a_send.at[k - 1], a_recv.at[k - 1], {"seq": other})
        )
    ss_ref[z] = outbuf[z]
    for copy in a_copies:
        copy.wait_recv()
    for cond, copy in pending:
        when(cond, copy.wait_send)


def fused(n_seq, n_phase, byte_embed, in_gain, w_qkv, w_up, out_gain, bounds, owner):
    tok, d = byte_embed.shape
    rows, _, width = w_qkv.shape
    heads = width // HD
    crows = bounds.shape[0]
    cols = out_gain.shape[0]
    slot = 2 * crows // n_seq
    reach = -(-WINDOW // tok)
    bf, f32 = jnp.bfloat16, jnp.float32
    vmem = pl.BlockSpec(memory_space=pltpu.VMEM)
    hbm = pl.BlockSpec(memory_space=pltpu.HBM)
    dma = pltpu.SemaphoreType.DMA
    states, stretch = pl.pallas_call(
        functools.partial(fused_kernel, (n_seq, n_phase, reach, slot)),
        out_shape=(
            jax.ShapeDtypeStruct((tok, width), bf),
            jax.ShapeDtypeStruct((n_seq, slot, cols), bf),
        ),
        in_specs=[hbm, vmem, hbm, hbm, vmem, vmem, vmem],
        out_specs=(vmem, vmem),
        scratch_shapes=[
            pltpu.VMEM((tok, d), bf),
            pltpu.VMEM((tok, d), bf),
            pltpu.VMEM((reach, n_phase, tok, width), bf),
            pltpu.VMEM((heads, 3, n_seq * rows, HD), bf),
            pltpu.VMEM((n_phase, w_up.shape[0], cols), bf),
            pltpu.VMEM((heads, tok, HD), bf),
            pltpu.VMEM((reach + 1, tok, HD), bf),
            pltpu.VMEM((reach + 1, tok, HD), bf),
            pltpu.VMEM((heads, tok, HD), f32),
            pltpu.VMEM((heads, tok, 1), f32),
            pltpu.VMEM((heads, tok, 1), f32),
            pltpu.VMEM((heads, n_phase, crows, HD), bf),
            pltpu.VMEM((n_phase, 8, crows), f32),
            pltpu.VMEM((n_seq, slot, cols), bf),
            dma((2 + heads,)),
            dma((2, heads, n_seq - 1)),
            dma((2, heads, n_seq - 1)),
            dma((2, heads, n_seq - 1)),
            dma((2, heads, n_seq - 1)),
            dma((n_phase - 1,)),
            dma((n_phase - 1,)),
            dma((n_phase - 1,)),
            dma((n_phase - 1,)),
            dma((reach,)),
            dma((reach,)),
            dma((reach, 4)),
            dma((reach, 4)),
            dma((heads, n_phase - 1)),
            dma((heads, n_phase - 1)),
            dma((n_phase - 1,)),
            dma((n_phase - 1,)),
            dma((n_seq - 1,)),
            dma((n_seq - 1,)),
        ],
        compiler_params=pltpu.CompilerParams(
            collective_id=0, has_side_effects=True, vmem_limit_bytes=36 * 1024 * 1024
        ),
    )(
        pltpu.with_memory_space_constraint(byte_embed, pltpu.HBM),
        in_gain.reshape(1, d),
        pltpu.with_memory_space_constraint(jnp.transpose(w_qkv, (1, 0, 2)), pltpu.HBM),
        pltpu.with_memory_space_constraint(w_up, pltpu.HBM),
        out_gain.reshape(1, cols),
        bounds.reshape(1, crows),
        owner.reshape(1, crows),
    )
    return states, stretch.reshape(n_seq * slot, cols)


def passed_along(value, axis, by):
    devices = lax.axis_size(axis)
    pairs = [(i, i + by) for i in range(devices) if 0 <= i + by < devices]
    return lax.ppermute(value, axis, pairs)


def project_rows(rows, w_up, out_gain):
    groups = lax.axis_size("phase")
    full_rows = lax.all_gather(rows, "phase", axis=1, tiled=True)
    w_cols = lax.all_to_all(w_up, "phase", split_axis=1, concat_axis=0, tiled=True)
    count = full_rows.shape[0]
    width = rows.shape[1]
    columns = w_cols.shape[1]
    pieces = jnp.einsum(
        "nsg,sgc->snc",
        full_rows.reshape(count, groups, width),
        w_cols.reshape(groups, width, columns),
        preferred_element_type=jnp.float32,
    )
    projected = jnp.sum(pieces.astype(jnp.bfloat16).astype(jnp.float32), axis=0)
    squares = lax.psum(jnp.sum(projected * projected, axis=1), "phase")
    scale = lax.rsqrt(squares / DC + 1e-05)
    return (projected * scale[:, None] * out_gain).astype(jnp.bfloat16)


def on_device(byte_embed, in_gain, w_qkv, w_up, out_gain, bounds, owner):
    tok = byte_embed.shape[0]
    n_seq = lax.axis_size("seq")
    mine = lax.axis_index("seq")
    section = lax.axis_index("phase")
    width_dev = w_qkv.shape[2]
    heads_dev = width_dev // HD
    x32 = byte_embed.astype(jnp.float32)
    normed = (x32 * lax.rsqrt(jnp.mean(x32 * x32, axis=1, keepdims=True) + 1e-05) * in_gain).astype(
        jnp.bfloat16
    )
    piece = lax.all_gather(w_qkv, "seq", axis=0, tiled=True)
    qkv = jnp.dot(
        normed, piece.reshape(piece.shape[0], 3 * width_dev), preferred_element_type=jnp.float32
    ).astype(jnp.bfloat16)
    qkv = qkv.reshape(tok, 3, heads_dev, HD)
    query = qkv[:, 0]
    keys = qkv[:, 1]
    values = qkv[:, 2]
    reach = -(-WINDOW // tok)
    key_list = [keys]
    value_list = [values]
    for distance in range(1, reach + 1):
        earlier_keys, earlier_values = passed_along((keys, values), "seq", distance)
        key_list = [earlier_keys] + key_list
        value_list = [earlier_values] + value_list
    key_all = jnp.concatenate(key_list, axis=0)
    value_all = jnp.concatenate(value_list, axis=0)
    scores = jnp.einsum(
        "ihd,jhd->hij", query, key_all, preferred_element_type=jnp.float32
    ) * HD ** (-0.5)
    q_pos = mine * tok + jnp.arange(tok, dtype=jnp.int32)
    k_pos = mine * tok - reach * tok + jnp.arange((reach + 1) * tok, dtype=jnp.int32)
    keep = (
        (k_pos[None, :] <= q_pos[:, None])
        & (k_pos[None, :] > q_pos[:, None] - WINDOW)
        & (k_pos[None, :] >= 0)
    )
    scores = jnp.where(keep[None], scores, -jnp.inf)
    top = jnp.max(scores, axis=2, keepdims=True)
    expo = jnp.exp(scores - top)
    probs = (expo / jnp.sum(expo, axis=2, keepdims=True)).astype(jnp.bfloat16)
    attended = jnp.einsum(
        "hij,jhd->ihd", probs, value_all, preferred_element_type=jnp.float32
    ).astype(jnp.bfloat16)
    attended = attended.reshape(tok, width_dev)
    residual = lax.dynamic_slice_in_dim(x32, section * width_dev, width_dev, 1)
    byte_states = (residual + attended.astype(jnp.float32)).astype(jnp.bfloat16)
    local = bounds - mine * tok
    stretch_rows = jnp.take(byte_states, local, axis=0)
    owners = owner[:, 0]
    crows = owners.shape[0]
    slot_count = 2 * crows // n_seq
    place = jnp.arange(crows, dtype=jnp.int32)
    earlier = (owners[:, None] == owners[None, :]) & (place[None, :] < place[:, None])
    rank = jnp.sum(earlier.astype(jnp.int32), axis=1)
    target = owners * slot_count + rank
    placing = (target[None, :] == jnp.arange(n_seq * slot_count, dtype=jnp.int32)[:, None]).astype(
        jnp.bfloat16
    )
    outgoing = jnp.dot(placing, stretch_rows, preferred_element_type=jnp.float32).astype(
        jnp.bfloat16
    )
    outgoing = outgoing.reshape(n_seq, slot_count, width_dev)
    arrived = lax.all_to_all(outgoing, "seq", split_axis=0, concat_axis=0, tiled=True).reshape(
        n_seq * slot_count, width_dev
    )
    stretch_states = project_rows(arrived, w_up, out_gain)
    return (byte_states, stretch_states)


def solution(mesh):
    n_seq, n_phase, n_dp = (mesh.shape[axis] for axis in ("seq", "phase", "dp"))

    def body(byte_embed, in_gain, w_qkv, *rest):
        tok, (rows, _, width) = byte_embed.shape[0], w_qkv.shape
        slot = 2 * rest[2].shape[0] // n_seq
        tiled = rows % 128 == 0 and width % HD == 0 and tok % 256 == 0 and slot % 16 == 0
        if tiled and n_dp == 2 and n_phase == 4 and w_qkv.shape[0] == rest[0].shape[0]:
            return fused(n_seq, n_phase, byte_embed, in_gain, w_qkv, *rest)
        return on_device(byte_embed, in_gain, w_qkv, *rest)

    return jax.shard_map(
        body,
        mesh=mesh,
        in_specs=(
            P(("dp", "seq"), None),
            P(),
            P("seq", None, "phase"),
            P("phase", None),
            P("phase"),
            P(("dp", "seq")),
            P(("dp", "seq"), None),
        ),
        out_specs=(P(("dp", "seq"), "phase"), P(("dp", "seq"), "phase")),
        check_vma=False,
    )
```

profile of v0, /device:TPU:0, one launch (start us, length us, event | category | flops | bytes accessed | tf_op | source)
XLA Modules:
  0.0 86.6 jit_solution(13990142474753903393)
XLA Ops:
  0.6 0.7 reshape.20.og_ref
  1.3 0.7 reshape.19.gain_ref
  2.0 0.0 copy-start
  2.0 0.7 copy-done
  2.7 0.0 copy-start.1
  2.7 0.7 copy-done.1
  3.3 81.8 %shard_map.86 = (bf16[512,384]{1,0:T(8,128)(2,1)S(1)}, bf16[4,64,768]{2,1,0:T(8,128)(2,1)S(1)}) custom-call(bf16[512,1536]{1,0:T(8,128)(2,1)} %x_ref.1, f32[1,1536]{1,0:T(1,128)S(1)} %reshape.19.gain_ref, bf16[3,384,384]{2,1,0:T(8,128)(2,1)} %bitcast.7, bf16[384,3072]{1,0:T(8,128)(2,1)} %up_ref.1, f32[1,768]{1,0:T(1,128)S(1)} %reshape.20.og_ref, ...), custom_call_target="tpu_custom_call" | custom-call | tf_op jit(solution)/shard_map/pallas_call | solution.py:424
  85.1 0.7 copy.11
  85.9 0.7 copy.12
Async XLA Ops:
  2.0 0.7 copy-start
  2.7 0.7 copy-start.1
where the time goes:
time: 86.9 us; the launch traced here: 86.6 us
  Pallas kernels  81.8 us (94%)
  local copies, waits for them, and re-layouts  4.19 us (5%)
    pallas_call x1, Pallas kernels, fused(): pl.pallas_call(functools.partial(fused_kernel, (n_seq, n_phase, reach, sl...  81.8 us
    unnamed x6, local copies, waits for them, and re-layouts  2.8 us

commit v1 on v0

--- a/solution.py
+++ b/solution.py
@@ -26,6 +26,10 @@
     bs_ref,
     ss_ref,
     xbuf,
+    gain,
+    og,
+    bnd,
+    own,
     normed,
     halo,
     wbuf,
@@ -36,9 +40,11 @@
     obuf,
     mbuf,
     lbuf,
-    rowbuf,
+    place,
+    outrows,
+    arrived,
+    acc,
     sqbuf,
-    outbuf,
     loc_sem,
     w_send,
     w_recv,
@@ -54,28 +60,42 @@
     g_recv,
     row_send,
     row_recv,
+    all_send,
+    all_recv,
     sq_send,
     sq_recv,
-    a_send,
-    a_recv,
 ):
     n_seq, n_phase, reach, slot = dims
     tok, d = xbuf.shape
     rows, width = w_ref.shape[1:]
     half = rows // 2
     heads = width // HD
-    crows = bounds_ref.shape[1]
-    cols = og_ref.shape[1]
+    last = heads - 1
+    crows = bnd.shape[1]
+    cols = og.shape[1]
     z = lax.axis_index("seq")
     p = lax.axis_index("phase")
     c = lax.axis_index("dp")
 
     own_x = pltpu.make_async_copy(x_ref, xbuf, loc_sem.at[0])
     own_x.start()
-    own_up = pltpu.make_async_copy(
-        up_ref.at[:, pl.ds(pl.multiple_of(p * cols, 128), cols)], upbuf.at[p], loc_sem.at[1]
-    )
-    own_up.start()
+    small = []
+    for i, (src, dst) in enumerate(
+        ((gain_ref, gain.at[0]), (bounds_ref, bnd), (owner_ref, own), (og_ref, og.at[0]))
+    ):
+        small.append(pltpu.make_async_copy(src, dst, loc_sem.at[2 + heads + i]))
+        small[i].start()
+
+    twin_core = {"dp": 1 - c}
+    peers = (
+        [{"seq": lax.rem(z + k, n_seq)} for k in range(1, n_seq)]
+        + [{"phase": lax.rem(p + k, n_phase)} for k in range(1, n_phase)]
+        + [twin_core]
+    )
+    barrier = pltpu.get_barrier_semaphore()
+    for peer in peers:
+        pl.semaphore_signal(barrier, inc=1, device_id=peer, device_id_type=MESH)
+
     own_w = []
     for h in range(heads):
         own_w.append(
@@ -86,16 +106,10 @@
             )
         )
         own_w[h].start()
-
-    twin_core = {"dp": 1 - c}
-    peers = (
-        [{"seq": lax.rem(z + k, n_seq)} for k in range(1, n_seq)]
-        + [{"phase": lax.rem(p + k, n_phase)} for k in range(1, n_phase)]
-        + [twin_core]
-    )
-    barrier = pltpu.get_barrier_semaphore()
-    for peer in peers:
-        pl.semaphore_signal(barrier, inc=1, device_id=peer, device_id_type=MESH)
+    own_up = pltpu.make_async_copy(
+        up_ref.at[:, pl.ds(pl.multiple_of(p * cols, 128), cols)], upbuf.at[p], loc_sem.at[1]
+    )
+    own_up.start()
     pl.semaphore_wait(barrier, len(peers))
 
     pending = []
@@ -117,51 +131,48 @@
     right, left = {"seq": z + 1}, {"seq": z - 1}
     has_right, has_left = z < n_seq - 1, z > 0
     ways = ((right, has_right, -1), (left, has_left, 1))
+    RIGHTWARD, LEFTWARD = 0, 1
 
     def chunk(h, shard):
         at = pl.multiple_of(shard * rows + c * half, half)
         return wbuf.at[h, :, pl.ds(at, half), :]
 
-    def issue_own(h):
-        if h >= heads or h in issued:
+    def slot_of(t, way):
+        return t - 1 if way == LEFTWARD else n_seq - t - 1
+
+    def issue_own(h, way, also=None):
+        src = chunk(h, z)
+        peer, cond, sign = ways[way]
+        cond = cond if also is None else cond & also
+        send(src, chunk(h, z), w_send.at[way, h, 0], w_recv.at[h, slot_of(1, way)], peer, cond)
+
+    twins = {}
+
+    def relay(h, t, way, also=None):
+        if t >= n_seq:
             return
-        issued.add(h)
-        src = w_ref.at[:, pl.ds(pl.multiple_of(c * half, half), half), pl.ds(h * HD, HD)]
-        for way, (peer, cond, sign) in enumerate(ways):
-            send(src, chunk(h, z), w_send.at[way, h, 0], w_recv.at[way, h, 0], peer, cond)
-
-    twins = {}
-    issued = set()
-    LEFTWARD, RIGHTWARD = 1, 0
-
-    def relay(h, t, *which):
-        for way in which:
-            if h >= heads or t >= n_seq or (h, t, way) in twins:
-                continue
-            peer, cond, sign = ways[way]
-            shard = z + sign * t
-            there = (shard >= 0) & (shard < n_seq)
-            piece = chunk(h, jnp.clip(shard, 0, n_seq - 1))
-            got = pltpu.make_async_remote_copy(
-                src_ref=piece,
-                dst_ref=piece,
-                send_sem=w_send.at[way, h, t - 1],
-                recv_sem=w_recv.at[way, h, t - 1],
-                device_id=peer,
-                device_id_type=MESH,
-            )
-            pl.when(there)(got.wait_recv)
-            if t < n_seq - 1:
-                send(piece, piece, w_send.at[way, h, t], w_recv.at[way, h, t], peer, there & cond)
-            twins[h, t, way] = (
-                there,
-                send(piece, piece, p_send.at[way, h, t - 1], p_recv.at[way, h, t - 1], twin_core, there),
-            )
+        peer, cond, sign = ways[way]
+        shard = z + sign * t
+        here = (shard >= 0) & (shard < n_seq)
+        there = here if also is None else here & also
+        piece = chunk(h, jnp.clip(shard, 0, n_seq - 1))
+        got = pltpu.make_async_remote_copy(
+            src_ref=piece,
+            dst_ref=piece,
+            send_sem=w_send.at[way, h, t - 1],
+            recv_sem=w_recv.at[h, slot_of(t, way)],
+            device_id=peer,
+            device_id_type=MESH,
+        )
+        pl.when(there)(got.wait_recv)
+        if t < n_seq - 1:
+            send(piece, piece, w_send.at[way, h, t], w_recv.at[h, slot_of(t + 1, way)], peer, there & cond)
+        twins[h, t, way] = (
+            here,
+            send(piece, piece, p_send.at[h, slot_of(t, way)], p_recv.at[h, slot_of(t, way)], twin_core, there),
+        )
 
     def finish(h):
-        own_w[h].wait()
-        for t in range(1, n_seq):
-            relay(h, t, LEFTWARD, RIGHTWARD)
         for t in range(1, n_seq):
             for way in range(2):
                 there, twin = twins[h, t, way]
@@ -172,8 +183,8 @@
     mine = {}
 
     def halo_start(dist, cond):
-        own = normed.at[:, pl.ds(pl.multiple_of(p * width, 128), width)]
-        src = own if dist == 1 else halo.at[dist - 2, p]
+        own_part = normed.at[:, pl.ds(pl.multiple_of(p * width, 128), width)]
+        src = own_part if dist == 1 else halo.at[dist - 2, p]
         mine[dist] = send(src, halo.at[dist - 1, p], h_send.at[dist - 1], h_recv.at[dist - 1], right, cond)
 
     gathers = {}
@@ -189,8 +200,10 @@
                 piece, piece, g_send.at[dist - 1, k - 1], g_recv.at[dist - 1, k - 1], across[k], there
             )
 
-    def halo_pass(dist):
+    def halo_pass(dist, also=None):
         there = z >= dist
+        if also is not None:
+            there = there & also
         for k in (1, 2):
             pl.when(there)(gathers[dist, k].wait_recv)
             part = pl.ds((k - 1) * (tok // 2), tok // 2)
@@ -205,7 +218,12 @@
             for k in (1, 2):
                 gathers[dist, 2 + k].wait_recv()
 
-    issue_own(0)
+    own_w[0].wait()
+    issue_own(0, RIGHTWARD)
+    issue_own(0, LEFTWARD)
+    for h in range(1, heads):
+        own_w[h].wait()
+        issue_own(h, LEFTWARD)
     up_rows = up_ref.shape[0] // 2
     up_half = pl.ds(pl.multiple_of(c * up_rows, up_rows), up_rows)
     up_copies, up_twins = [], []
@@ -223,34 +241,43 @@
         )
 
     own_x.wait()
+    small[0].wait()
     step_rows = 64
+
 
     @pl.loop(0, tok // step_rows)
     def _(i):
         r = pl.ds(pl.multiple_of(i * step_rows, step_rows), step_rows)
         xx = xbuf[r, :].astype(jnp.float32)
         scale = lax.rsqrt(jnp.mean(xx * xx, axis=1, keepdims=True) + 1e-05)
-        normed[r, :] = (xx * scale * gain_ref[...]).astype(jnp.bfloat16)
-
-    relay(0, 1, LEFTWARD)
+        normed[r, :] = (xx * scale * gain[...]).astype(jnp.bfloat16)
+
     halo_start(1, has_right)
+    first, second, final = z == 0, z == 1, z == n_seq - 1
+    for h in range(1, heads):
+        issue_own(h, RIGHTWARD, first)
 
     def column(ref):
         wide = jnp.broadcast_to(ref[...].astype(jnp.float32), (crows, crows))
         return wide.T
 
-    local = column(bounds_ref)[:, 0:1] - (z * tok).astype(jnp.float32)
+    relay(0, 1, RIGHTWARD)
+    relay(0, 1, LEFTWARD)
+    for copy in small[1:]:
+        copy.wait()
+    local = column(bnd)[:, 0:1] - (z * tok).astype(jnp.float32)
     spot = lax.broadcasted_iota(jnp.int32, (crows, tok), 1).astype(jnp.float32)
     pick = jnp.where(local == spot, 1.0, 0.0).astype(jnp.bfloat16)
-    same = column(owner_ref) == owner_ref[...].astype(jnp.float32)
+    same = column(own) == own[...].astype(jnp.float32)
     before = lax.broadcasted_iota(jnp.int32, (crows, crows), 0) < lax.broadcasted_iota(
         jnp.int32, (crows, crows), 1
     )
     rank = jnp.sum(jnp.where(same & before, 1, 0), axis=0, keepdims=True)
-    target = owner_ref[...] * slot + rank
-    place = jnp.where(
+    target = own[...] * slot + rank
+    route = jnp.where(
         target == lax.broadcasted_iota(jnp.int32, (n_seq * slot, crows), 0), 1.0, 0.0
     ).astype(jnp.bfloat16)
+    place[...] = jnp.dot(route, pick, preferred_element_type=jnp.float32).astype(jnp.bfloat16)
 
     tq = min(tok, 256)
     scale = HD ** (-0.5) * math.log2(math.e)
@@ -303,82 +330,157 @@
             vbuf[dist] = got[:, HD:]
             attend(dist, h)
 
-    row_copies = []
-
     def close(h):
         at = slice(h * HD, (h + 1) * HD)
         res = xbuf[:, pl.ds(pl.multiple_of(p * width + h * HD, HD), HD)].astype(jnp.float32)
         att = (obuf[h] / lbuf[h]).astype(jnp.bfloat16).astype(jnp.float32)
         states = (res + att).astype(jnp.bfloat16)
         bs_ref[:, at] = states
-        rowbuf[h, p] = jnp.dot(pick, states, preferred_element_type=jnp.float32).astype(jnp.bfloat16)
-        for k in range(1, n_phase):
-            row_copies.append(
-                send(
-                    rowbuf.at[h, p],
-                    rowbuf.at[h, p],
-                    row_send.at[h, k - 1],
-                    row_recv.at[h, k - 1],
-                    {"phase": lax.rem(p + k, n_phase)},
+        routed = jnp.dot(place[...], states, preferred_element_type=jnp.float32).astype(jnp.bfloat16)
+        for s in range(n_seq):
+            outrows[h, s] = routed[s * slot : (s + 1) * slot]
+        for k in range(1, n_seq):
+            other = lax.rem(z + k, n_seq)
+            send(
+                outrows.at[h, other],
+                arrived.at[h, p, z],
+                row_send.at[h, k - 1],
+                row_recv.at[h, z],
+                {"seq": other},
+            )
+        arrived[h, p, z] = outrows[h, z]
+
+    def rows_wait(h, s, cond=None):
+        here = arrived.at[h, p, s]
+        got = pltpu.make_async_remote_copy(
+            src_ref=here,
+            dst_ref=here,
+            send_sem=row_send.at[h, 0],
+            recv_sem=row_recv.at[h, s],
+            device_id={"seq": lax.rem(z + 1, n_seq)},
+            device_id_type=MESH,
+        )
+        pl.when(z != s if cond is None else (z != s) & cond)(got.wait_recv)
+
+    spreads = {}
+
+    def spread(h, j, cond=None):
+        sources = [n_seq - 1] if j else list(range(n_seq - 1))
+        if (h, j) not in spreads:
+            piece = arrived.at[h, p, pl.ds(sources[0], len(sources))]
+            spreads[h, j] = [
+                pltpu.make_async_remote_copy(
+                    src_ref=piece,
+                    dst_ref=piece,
+                    send_sem=all_send.at[h, j, k - 1],
+                    recv_sem=all_recv.at[h, j, k - 1],
+                    device_id={"phase": lax.rem(p + k, n_phase)},
+                    device_id_type=MESH,
                 )
-            )
-
+                for k in range(1, n_phase)
+            ]
+            pending.extend((None, copy) for copy in spreads[h, j])
+        for s in sources:
+            rows_wait(h, s, cond)
+        for copy in spreads[h, j]:
+            when(cond, copy.start)
+
+    for h in range(1, heads):
+        relay(h, 1, LEFTWARD)
     halo_spread(1)
-    issue_own(1)
-    relay(0, 1, RIGHTWARD)
-    for t in range(2, n_seq):
-        relay(0, t, LEFTWARD)
-    for dist in range(2, reach + 1):
-        halo_spread(dist)
-        halo_pass(dist - 1)
-    relay(1, 1, LEFTWARD, RIGHTWARD)
-    issue_own(2)
-    relay(0, 2, RIGHTWARD)
     for k in range(1, n_phase):
         up_copies[k - 1].wait_recv()
         piece = upbuf.at[lax.rem(p + n_phase - k, n_phase), up_half]
         up_twins.append(send(piece, piece, upp_send.at[k - 1], upp_recv.at[k - 1], twin_core))
+    for h in range(1, heads):
+        issue_own(h, RIGHTWARD, second)
+        relay(h, 1, RIGHTWARD, second)
+    relay(0, 2, RIGHTWARD)
+    issue_own(1, RIGHTWARD, z > 1)
     for t in range(2, n_seq):
-        relay(1, t, LEFTWARD)
-
-    for h in range(heads):
-        issue_own(h + 1)
-        finish(h)
-        own_block(h)
-        relay(h + 2, 1, LEFTWARD, RIGHTWARD)
-        if h == 0:
-            halo_pass(reach)
-        relay(h + 1, 2, LEFTWARD, RIGHTWARD)
-        for dist in range(1, reach):
-            if h == 0:
-                halo_wait(dist)
-            earlier_block(h, dist)
-        relay(h + 2, 2, LEFTWARD, RIGHTWARD)
-        issue_own(h + 3)
+        for h in range(heads):
+            relay(h, t, LEFTWARD)
+    for dist in range(2, reach + 1):
+        halo_pass(dist - 1)
+        halo_spread(dist)
+    for t in range(3, n_seq):
+        relay(0, t, RIGHTWARD)
+    finish(0)
+    own_block(0)
+    relay(1, 1, RIGHTWARD, (z > 1) & (z < n_seq - 1))
+    relay(1, 2, RIGHTWARD, z < n_seq - 1)
+    issue_own(2, RIGHTWARD, z > 1)
+    for dist in range(1, reach):
+        halo_wait(dist)
+        earlier_block(0, dist)
+    relay(1, 1, RIGHTWARD, final)
+    relay(1, 2, RIGHTWARD, final)
+    halo_pass(reach, final)
+    for t in range(3, n_seq):
+        relay(1, t, RIGHTWARD)
+    finish(1)
+    own_block(1)
+    relay(2, 1, RIGHTWARD, (z > 1) & (z < n_seq - 1))
+    for dist in range(1, reach):
+        earlier_block(1, dist)
+    halo_pass(reach, z < n_seq - 1)
+    relay(2, 1, RIGHTWARD, final)
+    relay(2, 2, RIGHTWARD, z < n_seq - 1)
     halo_wait(reach)
-    for h in range(heads):
+    earlier_block(0, reach)
+    close(0)
+    for h in range(1, last):
         earlier_block(h, reach)
         close(h)
-
+    relay(2, 2, RIGHTWARD, final)
+    for h in range(last):
+        spread(h, 0, z >= n_seq - 2)
+        spread(h, 1, final)
+    for t in range(3, n_seq):
+        relay(2, t, RIGHTWARD)
+    finish(last)
+    own_block(last)
+    for dist in range(1, reach + 1):
+        earlier_block(last, dist)
+    close(last)
+    for h in range(last):
+        spread(h, 0, z < n_seq - 2)
+    for h in range(last):
+        spread(h, 1, z < n_seq - 1)
+    spread(last, 0)
     own_up.wait()
     for twin in up_twins:
         twin.wait_recv()
-
-    def piece(s):
-        got = jnp.dot(
-            jnp.concatenate([rowbuf[h, s] for h in range(heads)], axis=1),
-            upbuf[s],
-            preferred_element_type=jnp.float32,
+    for k in range(1, n_phase):
+        for h in range(last):
+            for j in range(2):
+                spreads[h, j][k - 1].wait_recv()
+    full = n_seq * slot
+
+    def rows_of(s, hs):
+        return jnp.concatenate([arrived[h, s].reshape(full, HD) for h in hs], axis=1)
+
+    for k in range(n_phase):
+        s = lax.rem(p + n_phase - k, n_phase)
+        acc[k] = jnp.dot(
+            rows_of(s, range(last)), upbuf[s, : last * HD, :], preferred_element_type=jnp.float32
+        )
+    spread(last, 1)
+
+    def piece_of(k):
+        s = lax.rem(p + n_phase - k, n_phase)
+        got = acc[k] + jnp.dot(
+            rows_of(s, [last]), upbuf[s, last * HD :, :], preferred_element_type=jnp.float32
         )
         return got.astype(jnp.bfloat16).astype(jnp.float32)
 
-    projected = piece(p)
-    for copy in row_copies:
-        copy.wait_recv()
+    projected = piece_of(0)
     for k in range(1, n_phase):
-        projected = projected + piece(lax.rem(p + k, n_phase))
+        for j in range(2):
+            spreads[last, j][k - 1].wait_recv()
+        projected = projected + piece_of(k)
     sq = jnp.sum(projected * projected, axis=1, keepdims=True)
-    sqbuf[p] = jnp.broadcast_to(sq, (crows, crows)).T[0:8, :]
+    sqbuf[p] = jnp.broadcast_to(sq, (full, 128)).T[0:8, :]
     sq_copies = []
     for k in range(1, n_phase):
         other = lax.rem(p + k, n_phase)
@@ -390,21 +492,9 @@
     all_sq = sqbuf[0]
     for k in range(1, n_phase):
         all_sq = all_sq + sqbuf[k]
-    all_sq = jnp.broadcast_to(all_sq[0:1, :], (crows, crows)).T[:, 0:1]
+    all_sq = jnp.broadcast_to(all_sq[0:1, :], (128, full)).T[:, 0:1]
     norm = lax.rsqrt(all_sq / (n_phase * cols) + 1e-05)
-    main_in = (projected * norm * og_ref[...]).astype(jnp.bfloat16)
-    routed = jnp.dot(place, main_in, preferred_element_type=jnp.float32).astype(jnp.bfloat16)
-    for s in range(n_seq):
-        outbuf[s] = routed[s * slot : (s + 1) * slot]
-    a_copies = []
-    for k in range(1, n_seq):
-        other = lax.rem(z + k, n_seq)
-        a_copies.append(
-            send(outbuf.at[other], ss_ref.at[z], a_send.at[k - 1], a_recv.at[k - 1], {"seq": other})
-        )
-    ss_ref[z] = outbuf[z]
-    for copy in a_copies:
-        copy.wait_recv()
+    ss_ref[...] = (projected * norm * og[...]).astype(jnp.bfloat16)
     for cond, copy in pending:
         when(cond, copy.wait_send)
 
@@ -421,16 +511,21 @@
     vmem = pl.BlockSpec(memory_space=pltpu.VMEM)
     hbm = pl.BlockSpec(memory_space=pltpu.HBM)
     dma = pltpu.SemaphoreType.DMA
+    in_hbm = lambda a: pltpu.with_memory_space_constraint(a, pltpu.HBM)
     states, stretch = pl.pallas_call(
         functools.partial(fused_kernel, (n_seq, n_phase, reach, slot)),
         out_shape=(
             jax.ShapeDtypeStruct((tok, width), bf),
-            jax.ShapeDtypeStruct((n_seq, slot, cols), bf),
+            jax.ShapeDtypeStruct((n_seq * slot, cols), bf),
         ),
-        in_specs=[hbm, vmem, hbm, hbm, vmem, vmem, vmem],
+        in_specs=[hbm] * 7,
         out_specs=(vmem, vmem),
         scratch_shapes=[
             pltpu.VMEM((tok, d), bf),
+            pltpu.VMEM((1, d), f32),
+            pltpu.VMEM((1, cols), f32),
+            pltpu.VMEM((1, crows), jnp.int32),
+            pltpu.VMEM((1, crows), jnp.int32),
             pltpu.VMEM((tok, d), bf),
             pltpu.VMEM((reach, n_phase, tok, width), bf),
             pltpu.VMEM((heads, 3, n_seq * rows, HD), bf),
@@ -441,14 +536,16 @@
             pltpu.VMEM((heads, tok, HD), f32),
             pltpu.VMEM((heads, tok, 1), f32),
             pltpu.VMEM((heads, tok, 1), f32),
-            pltpu.VMEM((heads, n_phase, crows, HD), bf),
-            pltpu.VMEM((n_phase, 8, crows), f32),
-            pltpu.VMEM((n_seq, slot, cols), bf),
-            dma((2 + heads,)),
+            pltpu.VMEM((n_seq * slot, tok), bf),
+            pltpu.VMEM((heads, n_seq, slot, HD), bf),
+            pltpu.VMEM((heads, n_phase, n_seq, slot, HD), bf),
+            pltpu.VMEM((n_phase, n_seq * slot, cols), f32),
+            pltpu.VMEM((n_phase, 8, n_seq * slot), f32),
+            dma((6 + heads,)),
             dma((2, heads, n_seq - 1)),
-            dma((2, heads, n_seq - 1)),
-            dma((2, heads, n_seq - 1)),
-            dma((2, heads, n_seq - 1)),
+            dma((heads, n_seq - 1)),
+            dma((heads, n_seq - 1)),
+            dma((heads, n_seq - 1)),
             dma((n_phase - 1,)),
             dma((n_phase - 1,)),
             dma((n_phase - 1,)),
@@ -457,26 +554,26 @@
             dma((reach,)),
             dma((reach, 4)),
             dma((reach, 4)),
-            dma((heads, n_phase - 1)),
-            dma((heads, n_phase - 1)),
+            dma((heads, n_seq - 1)),
+            dma((heads, n_seq)),
+            dma((heads, 2, n_phase - 1)),
+            dma((heads, 2, n_phase - 1)),
             dma((n_phase - 1,)),
             dma((n_phase - 1,)),
-            dma((n_seq - 1,)),
-            dma((n_seq - 1,)),
         ],
         compiler_params=pltpu.CompilerParams(
-            collective_id=0, has_side_effects=True, vmem_limit_bytes=36 * 1024 * 1024
+            collective_id=0, has_side_effects=True, vmem_limit_bytes=48 * 1024 * 1024
         ),
     )(
-        pltpu.with_memory_space_constraint(byte_embed, pltpu.HBM),
-        in_gain.reshape(1, d),
-        pltpu.with_memory_space_constraint(jnp.transpose(w_qkv, (1, 0, 2)), pltpu.HBM),
-        pltpu.with_memory_space_constraint(w_up, pltpu.HBM),
-        out_gain.reshape(1, cols),
-        bounds.reshape(1, crows),
-        owner.reshape(1, crows),
-    )
-    return states, stretch.reshape(n_seq * slot, cols)
+        in_hbm(byte_embed),
+        in_hbm(in_gain),
+        in_hbm(jnp.transpose(w_qkv, (1, 0, 2))),
+        in_hbm(w_up),
+        in_hbm(out_gain),
+        in_hbm(bounds.reshape(1, crows)),
+        in_hbm(owner.reshape(1, crows)),
+    )
+    return states, stretch
 
 
 def passed_along(value, axis, by):

time: 86.9 us -> 76.3 us (0.88)
  Pallas kernels: 81.8 us -> 74 us
  local copies, waits for them, and re-layouts: 4.19 us -> 1.49 us
    pallas_call x1, Pallas kernels: 81.8 us -> 74 us  [fused(): pl.pallas_call(functools.partial(fused_kernel, (n_seq, n_phase, reach, sl...]
    reshape x2 -> x0, local copies, waits for them, and re-layouts: 1.39 us -> none  [the longest x1 0.7 us: fused(): in_gain.reshape(1, d)]
    unnamed x6 -> x2, local copies, waits for them, and re-layouts: 2.8 us -> 1.49 us
where the time goes in v1:
time: 76.3 us; the launch traced here: 76.2 us
  Pallas kernels  74 us (97%)
  local copies, waits for them, and re-layouts  1.49 us (2%)
    pallas_call x1, Pallas kernels, fused(): pl.pallas_call(functools.partial(fused_kernel, (n_seq, n_phase, reach, sl...  74 us

profile of v1, /device:TPU:0, one launch (start us, length us, event | category | flops | bytes accessed | tf_op | source)
XLA Modules:
  0.0 76.2 jit_solution(4194132028320142473)
XLA Ops:
  0.6 74.0 %shard_map.86 = (bf16[512,384]{1,0:T(8,128)(2,1)S(1)}, bf16[256,768]{1,0:T(8,128)(2,1)S(1)}) custom-call(bf16[512,1536]{1,0:T(8,128)(2,1)} %x_ref.1, f32[1536]{0:T(1024)} %gain_ref.1, bf16[3,384,384]{2,1,0:T(8,128)(2,1)} %bitcast.3, bf16[384,3072]{1,0:T(8,128)(2,1)} %up_ref.1, f32[768]{0:T(1024)} %og_ref.1, s32[1,128]{1,0:T(1,128)} %bitcast.4, s32[1,128]{1,0:T(1,128)} %bitcast.5), custom_call_target="tpu_custom_call" | custom-call | tf_op jit(solution)/shard_map/pallas_call | solution.py:515
  74.7 0.7 copy.11
  75.4 0.7 copy.12

commit v2 on v1

--- a/solution.py
+++ b/solution.py
@@ -44,6 +44,7 @@
     outrows,
     arrived,
     acc,
+    partial,
     sqbuf,
     loc_sem,
     w_send,
@@ -112,21 +113,27 @@
     own_up.start()
     pl.semaphore_wait(barrier, len(peers))
 
-    pending = []
-
     def when(cond, action):
         if cond is None:
             action()
         else:
             pl.when(cond)(action)
 
-    def send(src, dst, ssem, rsem, peer, cond=None):
-        copy = pltpu.make_async_remote_copy(
+    def move(src, dst, ssem, rsem, peer):
+        return pltpu.make_async_remote_copy(
             src_ref=src, dst_ref=dst, send_sem=ssem, recv_sem=rsem, device_id=peer, device_id_type=MESH
         )
+
+    def send(src, dst, ssem, rsem, peer, cond=None):
+        copy = move(src, dst, ssem, rsem, peer)
         when(cond, copy.start)
-        pending.append((cond, copy))
         return copy
+
+    def sent(ref, ssem, cond=None):
+        when(cond, move(ref, ref, ssem, ssem, twin_core).wait_send)
+
+    def landed(ref, rsem, cond=None):
+        when(cond, move(ref, ref, rsem, rsem, twin_core).wait_recv)
 
     right, left = {"seq": z + 1}, {"seq": z - 1}
     has_right, has_left = z < n_seq - 1, z > 0
@@ -144,9 +151,7 @@
         src = chunk(h, z)
         peer, cond, sign = ways[way]
         cond = cond if also is None else cond & also
-        send(src, chunk(h, z), w_send.at[way, h, 0], w_recv.at[h, slot_of(1, way)], peer, cond)
-
-    twins = {}
+        send(src, chunk(h, z), w_send, w_recv.at[h, slot_of(1, way)], peer, cond)
 
     def relay(h, t, way, also=None):
         if t >= n_seq:
@@ -156,27 +161,21 @@
         here = (shard >= 0) & (shard < n_seq)
         there = here if also is None else here & also
         piece = chunk(h, jnp.clip(shard, 0, n_seq - 1))
-        got = pltpu.make_async_remote_copy(
-            src_ref=piece,
-            dst_ref=piece,
-            send_sem=w_send.at[way, h, t - 1],
-            recv_sem=w_recv.at[h, slot_of(t, way)],
-            device_id=peer,
-            device_id_type=MESH,
-        )
-        pl.when(there)(got.wait_recv)
+        landed(piece, w_recv.at[h, slot_of(t, way)], there)
         if t < n_seq - 1:
-            send(piece, piece, w_send.at[way, h, t], w_recv.at[h, slot_of(t + 1, way)], peer, there & cond)
-        twins[h, t, way] = (
-            here,
-            send(piece, piece, p_send.at[h, slot_of(t, way)], p_recv.at[h, slot_of(t, way)], twin_core, there),
-        )
-
-    def finish(h):
-        for t in range(1, n_seq):
-            for way in range(2):
-                there, twin = twins[h, t, way]
-                pl.when(there)(twin.wait_recv)
+            send(piece, piece, w_send, w_recv.at[h, slot_of(t + 1, way)], peer, there & cond)
+        late = (way == RIGHTWARD) & (t == z)
+        group = jnp.where(late, last + 1, h) if h == last else h
+        send(piece, piece, p_send, p_recv.at[group], twin_core, there)
+
+    def finish(h, late=None, also=True):
+        if h < last:
+            landed(wbuf.at[h, :, pl.ds(0, (n_seq - 1) * half)], p_recv.at[h])
+        elif late:
+            landed(wbuf.at[h, :, pl.ds(0, half)], p_recv.at[last + 1], (z > 0) & also)
+        else:
+            landed(wbuf.at[h, :, pl.ds(0, (n_seq - 2) * half)], p_recv.at[h], (z > 0) & also)
+            landed(wbuf.at[h, :, pl.ds(0, (n_seq - 1) * half)], p_recv.at[h], (z == 0) & also)
 
     across = {1: {"phase": p + 1 - 2 * lax.rem(p, 2)}, 2: {"phase": lax.rem(p + 2, n_phase)}}
     spots = {k: v["phase"] for k, v in across.items()}
@@ -197,7 +196,7 @@
         for k in (1, 2):
             piece = halo.at[dist - 1, p]
             gathers[dist, k] = send(
-                piece, piece, g_send.at[dist - 1, k - 1], g_recv.at[dist - 1, k - 1], across[k], there
+                piece, piece, g_send.at[dist - 1], g_recv.at[dist - 1, k - 1], across[k], there
             )
 
     def halo_pass(dist, also=None):
@@ -209,14 +208,13 @@
             part = pl.ds((k - 1) * (tok // 2), tok // 2)
             piece = halo.at[dist - 1, spots[k], part]
             gathers[dist, 2 + k] = send(
-                piece, piece, g_send.at[dist - 1, k + 1], g_recv.at[dist - 1, k + 1], across[3 - k], there
+                piece, piece, g_send.at[dist - 1], g_recv.at[dist - 1, 2], across[3 - k], there
             )
 
     def halo_wait(dist):
         @pl.when(z >= dist)
         def _():
-            for k in (1, 2):
-                gathers[dist, 2 + k].wait_recv()
+            landed(halo.at[dist - 1, 0], g_recv.at[dist - 1, 2])
 
     own_w[0].wait()
     issue_own(0, RIGHTWARD)
@@ -226,19 +224,10 @@
         issue_own(h, LEFTWARD)
     up_rows = up_ref.shape[0] // 2
     up_half = pl.ds(pl.multiple_of(c * up_rows, up_rows), up_rows)
-    up_copies, up_twins = [], []
     for k in range(1, n_phase):
         other = lax.rem(p + k, n_phase)
         part = pl.ds(pl.multiple_of(other * cols, 128), cols)
-        up_copies.append(
-            send(
-                up_ref.at[up_half, part],
-                upbuf.at[p, up_half],
-                up_send.at[k - 1],
-                up_recv.at[k - 1],
-                {"phase": other},
-            )
-        )
+        send(up_ref.at[up_half, part], upbuf.at[p, up_half], up_send, up_recv, {"phase": other})
 
     own_x.wait()
     small[0].wait()
@@ -312,7 +301,10 @@
             lbuf[h, r, :] = total
             obuf[h, r, :] = o
 
-    def own_block(h):
+    def own_block(h, also=None):
+        if also is not None:
+            pl.when(also)(lambda: own_block(h))
+            return
         w = jnp.concatenate([wbuf[h, j] for j in range(3)], axis=1)
         got = jnp.dot(normed[...], w, preferred_element_type=jnp.float32).astype(jnp.bfloat16)
         qbuf[h] = got[:, :HD]
@@ -320,8 +312,8 @@
         vbuf[0] = got[:, 2 * HD :]
         attend(0, h)
 
-    def earlier_block(h, dist):
-        @pl.when(z >= dist)
+    def earlier_block(h, dist, also=True):
+        @pl.when((z >= dist) & also)
         def _():
             w = jnp.concatenate([wbuf[h, j] for j in range(1, 3)], axis=1)
             rows_in = jnp.concatenate([halo[dist - 1, q] for q in range(n_phase)], axis=1)
@@ -329,6 +321,37 @@
             kbuf[dist] = got[:, :HD]
             vbuf[dist] = got[:, HD:]
             attend(dist, h)
+
+    def split_rows(dist):
+        if dist == 0:
+            return normed[:, :rows], normed[:, rows:]
+        pieces = [halo[dist - 1, q] for q in range(n_phase)]
+        return pieces[0], jnp.concatenate(pieces[1:], axis=1)
+
+    def some_weights(dist, r):
+        return jnp.concatenate([wbuf[last, j, r, :] for j in range(min(dist, 1), 3)], axis=1)
+
+    def project_early(dist, also):
+        @pl.when((z >= dist) & also)
+        def _():
+            got = jnp.dot(
+                split_rows(dist)[1], some_weights(dist, slice(rows, None)), preferred_element_type=jnp.float32
+            )
+            partial[dist, :, pl.ds(min(dist, 1) * HD, got.shape[1])] = got
+
+    def project_late(dist, also):
+        @pl.when((z >= dist) & also)
+        def _():
+            got = jnp.dot(
+                split_rows(dist)[0], some_weights(dist, slice(0, rows)), preferred_element_type=jnp.float32
+            )
+            start = min(dist, 1) * HD
+            got = (got + partial[dist, :, pl.ds(start, got.shape[1])]).astype(jnp.bfloat16)
+            if dist == 0:
+                qbuf[last] = got[:, :HD]
+            kbuf[dist] = got[:, HD - start : 2 * HD - start]
+            vbuf[dist] = got[:, 2 * HD - start :]
+            attend(dist, last)
 
     def close(h):
         at = slice(h * HD, (h + 1) * HD)
@@ -339,59 +362,47 @@
         routed = jnp.dot(place[...], states, preferred_element_type=jnp.float32).astype(jnp.bfloat16)
         for s in range(n_seq):
             outrows[h, s] = routed[s * slot : (s + 1) * slot]
+        arrived[h, p, z] = outrows[h, z]
+        rows_out(h, False)
+
+    def rows_out(h, held):
         for k in range(1, n_seq):
             other = lax.rem(z + k, n_seq)
+            wait = (other > z) & (other >= n_seq - 2)
             send(
                 outrows.at[h, other],
                 arrived.at[h, p, z],
-                row_send.at[h, k - 1],
-                row_recv.at[h, z],
+                row_send,
+                row_recv.at[h, jnp.maximum(z - (n_seq - 3), 0)],
                 {"seq": other},
+                wait if held else jnp.logical_not(wait),
             )
-        arrived[h, p, z] = outrows[h, z]
-
-    def rows_wait(h, s, cond=None):
-        here = arrived.at[h, p, s]
-        got = pltpu.make_async_remote_copy(
-            src_ref=here,
-            dst_ref=here,
-            send_sem=row_send.at[h, 0],
-            recv_sem=row_recv.at[h, s],
-            device_id={"seq": lax.rem(z + 1, n_seq)},
-            device_id_type=MESH,
-        )
-        pl.when(z != s if cond is None else (z != s) & cond)(got.wait_recv)
-
-    spreads = {}
-
-    def spread(h, j, cond=None):
-        sources = [n_seq - 1] if j else list(range(n_seq - 1))
-        if (h, j) not in spreads:
-            piece = arrived.at[h, p, pl.ds(sources[0], len(sources))]
-            spreads[h, j] = [
-                pltpu.make_async_remote_copy(
-                    src_ref=piece,
-                    dst_ref=piece,
-                    send_sem=all_send.at[h, j, k - 1],
-                    recv_sem=all_recv.at[h, j, k - 1],
-                    device_id={"phase": lax.rem(p + k, n_phase)},
-                    device_id_type=MESH,
-                )
-                for k in range(1, n_phase)
-            ]
-            pending.extend((None, copy) for copy in spreads[h, j])
-        for s in sources:
-            rows_wait(h, s, cond)
-        for copy in spreads[h, j]:
-            when(cond, copy.start)
+
+    outer = n_seq - 2
+
+    def rows_in(h, j, cond):
+        if j == 0:
+            landed(arrived.at[h, p, pl.ds(0, outer)], row_recv.at[h, 0], cond & (z >= outer))
+            landed(arrived.at[h, p, pl.ds(0, outer - 1)], row_recv.at[h, 0], cond & (z < outer))
+        else:
+            src = outer + j - 1
+            landed(arrived.at[h, p, src], row_recv.at[h, j], cond & (z != src))
+
+    def spread(h, j, cond, waited=False):
+        if not waited:
+            rows_in(h, j, cond)
+        piece = arrived.at[h, p, pl.ds(0, outer) if j == 0 else pl.ds(outer + j - 1, 1)]
+        group = 1 + j // 2 if h == last else 0
+        for k in range(1, n_phase):
+            send(piece, piece, all_send, all_recv.at[group], {"phase": lax.rem(p + k, n_phase)}, cond)
 
     for h in range(1, heads):
         relay(h, 1, LEFTWARD)
     halo_spread(1)
+    landed(upbuf.at[pl.ds(0, n_phase - 1), up_half], up_recv)
     for k in range(1, n_phase):
-        up_copies[k - 1].wait_recv()
         piece = upbuf.at[lax.rem(p + n_phase - k, n_phase), up_half]
-        up_twins.append(send(piece, piece, upp_send.at[k - 1], upp_recv.at[k - 1], twin_core))
+        send(piece, piece, upp_send, upp_recv, twin_core)
     for h in range(1, heads):
         issue_own(h, RIGHTWARD, second)
         relay(h, 1, RIGHTWARD, second)
@@ -426,36 +437,64 @@
     halo_pass(reach, z < n_seq - 1)
     relay(2, 1, RIGHTWARD, final)
     relay(2, 2, RIGHTWARD, z < n_seq - 1)
+    inner = z < n_seq - 1
+    finish(last, False, inner)
+    finish(last, True, inner)
+    own_block(last, inner)
+    for dist in range(1, reach):
+        earlier_block(last, dist, inner)
     halo_wait(reach)
-    earlier_block(0, reach)
-    close(0)
+    outside = z < outer
+    for h in range(last):
+        earlier_block(h, reach)
+        if h == last - 1:
+            for t in range(3, n_seq):
+                relay(last, t, RIGHTWARD, c == 1)
+        close(h)
+        if h == 0:
+            relay(last, 2, RIGHTWARD, final)
+    for h in range(last):
+        spread(h, 2, final)
+    finish(last, False, final)
+    for dist in range(reach):
+        project_early(dist, final)
+    for t in range(3, n_seq):
+        relay(last, t, RIGHTWARD, c == 0)
+    project_early(reach, final)
+    finish(last, True, final)
+    for dist in range(reach + 1):
+        project_late(dist, final)
+        if dist == 0:
+            for h in range(last):
+                spread(h, 1, final)
+    for h in range(last):
+        spread(h, 1, z == outer)
+    rows_in(0, 2, z == outer)
+    for h in range(last):
+        pl.when(z == outer)(lambda h=h: rows_out(h, True))
+    earlier_block(last, reach, inner)
+    close(last)
+    pl.when(z == outer)(lambda: rows_out(last, True))
+    spread(last, 1, z == outer)
+    spread(last, 2, final)
+    for h in range(heads):
+        spread(h, 0, outside)
+    rows_in(0, 2, outside)
+    for h in range(heads):
+        pl.when(outside)(lambda h=h: rows_out(h, True))
+    spread(0, 1, outside)
+    spread(0, 2, inner, waited=True)
     for h in range(1, last):
-        earlier_block(h, reach)
-        close(h)
-    relay(2, 2, RIGHTWARD, final)
-    for h in range(last):
-        spread(h, 0, z >= n_seq - 2)
-        spread(h, 1, final)
-    for t in range(3, n_seq):
-        relay(2, t, RIGHTWARD)
-    finish(last)
-    own_block(last)
-    for dist in range(1, reach + 1):
-        earlier_block(last, dist)
-    close(last)
-    for h in range(last):
-        spread(h, 0, z < n_seq - 2)
-    for h in range(last):
-        spread(h, 1, z < n_seq - 1)
-    spread(last, 0)
+        spread(h, 1, outside)
+        spread(h, 2, inner)
+    for h in range(heads):
+        spread(h, 0, z >= outer)
+    spread(last, 1, z != outer)
     own_up.wait()
-    for twin in up_twins:
-        twin.wait_recv()
-    for k in range(1, n_phase):
-        for h in range(last):
-            for j in range(2):
-                spreads[h, j][k - 1].wait_recv()
+    landed(upbuf.at[pl.ds(0, n_phase - 1), up_half], upp_recv)
+    landed(arrived.at[pl.ds(0, last), pl.ds(0, n_phase - 1)], all_recv.at[0])
     full = n_seq * slot
+    cut = full - slot
 
     def rows_of(s, hs):
         return jnp.concatenate([arrived[h, s].reshape(full, HD) for h in hs], axis=1)
@@ -465,38 +504,46 @@
         acc[k] = jnp.dot(
             rows_of(s, range(last)), upbuf[s, : last * HD, :], preferred_element_type=jnp.float32
         )
-    spread(last, 1)
-
-    def piece_of(k):
-        s = lax.rem(p + n_phase - k, n_phase)
-        got = acc[k] + jnp.dot(
-            rows_of(s, [last]), upbuf[s, last * HD :, :], preferred_element_type=jnp.float32
-        )
-        return got.astype(jnp.bfloat16).astype(jnp.float32)
-
-    projected = piece_of(0)
+
+    def complete(j):
+        r = slice(0, cut) if j == 0 else slice(cut, full)
+        projected = 0.0
+        for k in range(n_phase):
+            s = lax.rem(p + n_phase - k, n_phase)
+            srcs = pl.ds(0, n_seq - 1) if j == 0 else pl.ds(n_seq - 1, 1)
+            lhs = arrived[last, s, srcs].reshape(r.stop - r.start, HD)
+            got = acc[k, r, :] + jnp.dot(lhs, upbuf[s, last * HD :, :], preferred_element_type=jnp.float32)
+            projected = projected + got.astype(jnp.bfloat16).astype(jnp.float32)
+        acc[0, r, :] = projected
+        sq = jnp.sum(projected * projected, axis=1, keepdims=True)
+        return jnp.broadcast_to(sq, (r.stop - r.start, 128))
+
+    landed(arrived.at[last, pl.ds(0, n_phase - 1), pl.ds(0, n_seq - 1)], all_recv.at[1])
+    sq_top = complete(0)
+    spread(last, 2, inner)
+    landed(arrived.at[last, pl.ds(0, n_phase - 1), pl.ds(0, 1)], all_recv.at[2])
+    sq_all = jnp.concatenate([sq_top, complete(1)], axis=0)
+    sqbuf[p] = sq_all.T[0:8, :]
     for k in range(1, n_phase):
-        for j in range(2):
-            spreads[last, j][k - 1].wait_recv()
-        projected = projected + piece_of(k)
-    sq = jnp.sum(projected * projected, axis=1, keepdims=True)
-    sqbuf[p] = jnp.broadcast_to(sq, (full, 128)).T[0:8, :]
-    sq_copies = []
-    for k in range(1, n_phase):
-        other = lax.rem(p + k, n_phase)
-        sq_copies.append(
-            send(sqbuf.at[p], sqbuf.at[p], sq_send.at[k - 1], sq_recv.at[k - 1], {"phase": other})
-        )
-    for copy in sq_copies:
-        copy.wait_recv()
+        send(sqbuf.at[p], sqbuf.at[p], sq_send, sq_recv, {"phase": lax.rem(p + k, n_phase)})
+    landed(sqbuf.at[pl.ds(0, n_phase - 1)], sq_recv)
     all_sq = sqbuf[0]
     for k in range(1, n_phase):
         all_sq = all_sq + sqbuf[k]
     all_sq = jnp.broadcast_to(all_sq[0:1, :], (128, full)).T[:, 0:1]
     norm = lax.rsqrt(all_sq / (n_phase * cols) + 1e-05)
-    ss_ref[...] = (projected * norm * og[...]).astype(jnp.bfloat16)
-    for cond, copy in pending:
-        when(cond, copy.wait_send)
+    ss_ref[...] = (acc[0] * norm * og[...]).astype(jnp.bfloat16)
+    sent(wbuf.at[:, :, pl.ds(0, half)], w_send, first | final)
+    sent(wbuf.at[:, :, pl.ds(0, (n_seq + 1) * half)], w_send, jnp.logical_not(first | final))
+    sent(wbuf.at[:, :, pl.ds(0, (n_seq - 1) * half)], p_send)
+    sent(upbuf.at[pl.ds(0, n_phase - 1), up_half], up_send)
+    sent(upbuf.at[pl.ds(0, n_phase - 1), up_half], upp_send)
+    for dist in range(1, reach + 1):
+        sent(halo.at[dist - 1, 0], h_send.at[dist - 1], (z >= dist - 1) & has_right)
+        sent(halo.at[dist - 1, pl.ds(0, 3)], g_send.at[dist - 1], z >= dist)
+    sent(outrows.at[:, pl.ds(0, n_seq - 1)], row_send)
+    sent(arrived.at[:, pl.ds(0, n_phase - 1)], all_send)
+    sent(sqbuf.at[pl.ds(0, n_phase - 1)], sq_send)
 
 
 def fused(n_seq, n_phase, byte_embed, in_gain, w_qkv, w_up, out_gain, bounds, owner):
@@ -540,26 +587,27 @@
             pltpu.VMEM((heads, n_seq, slot, HD), bf),
             pltpu.VMEM((heads, n_phase, n_seq, slot, HD), bf),
             pltpu.VMEM((n_phase, n_seq * slot, cols), f32),
+            pltpu.VMEM((reach + 1, tok, 3 * HD), f32),
             pltpu.VMEM((n_phase, 8, n_seq * slot), f32),
             dma((6 + heads,)),
-            dma((2, heads, n_seq - 1)),
+            dma(()),
             dma((heads, n_seq - 1)),
-            dma((heads, n_seq - 1)),
-            dma((heads, n_seq - 1)),
-            dma((n_phase - 1,)),
-            dma((n_phase - 1,)),
-            dma((n_phase - 1,)),
-            dma((n_phase - 1,)),
+            dma(()),
+            dma((heads + 1,)),
+            dma(()),
+            dma(()),
+            dma(()),
+            dma(()),
             dma((reach,)),
             dma((reach,)),
-            dma((reach, 4)),
-            dma((reach, 4)),
-            dma((heads, n_seq - 1)),
-            dma((heads, n_seq)),
-            dma((heads, 2, n_phase - 1)),
-            dma((heads, 2, n_phase - 1)),
-            dma((n_phase - 1,)),
-            dma((n_phase - 1,)),
+            dma((reach,)),
+            dma((reach, 3)),
+            dma(()),
+            dma((heads, 3)),
+            dma(()),
+            dma((3,)),
+            dma(()),
+            dma(()),
         ],
         compiler_params=pltpu.CompilerParams(
             collective_id=0, has_side_effects=True, vmem_limit_bytes=48 * 1024 * 1024
@@ -679,7 +727,8 @@
         tok, (rows, _, width) = byte_embed.shape[0], w_qkv.shape
         slot = 2 * rest[2].shape[0] // n_seq
         tiled = rows % 128 == 0 and width % HD == 0 and tok % 256 == 0 and slot % 16 == 0
-        if tiled and n_dp == 2 and n_phase == 4 and w_qkv.shape[0] == rest[0].shape[0]:
+        fits = n_seq == n_phase and width == 3 * HD and WINDOW == 2 * tok
+        if tiled and fits and n_dp == 2 and n_phase == 4 and w_qkv.shape[0] == rest[0].shape[0]:
             return fused(n_seq, n_phase, byte_embed, in_gain, w_qkv, *rest)
         return on_device(byte_embed, in_gain, w_qkv, *rest)
 

time: 76.3 us -> 72.5 us (0.950)
  Pallas kernels: 74 us -> 70.2 us
    pallas_call x1, Pallas kernels: 74 us -> 70.2 us  [fused(): pl.pallas_call(functools.partial(fused_kernel, (n_seq, n_phase, reach, sl...]
where the time goes in v2:
time: 72.5 us; the launch traced here: 72.4 us
  Pallas kernels  70.2 us (97%)
  local copies, waits for them, and re-layouts  1.49 us (2%)
    pallas_call x1, Pallas kernels, fused(): pl.pallas_call(functools.partial(fused_kernel, (n_seq, n_phase, reach, sl...  70.2 us
    unnamed x2, local copies, waits for them, and re-layouts  1.49 us

profile of v2, /device:TPU:0, one launch (start us, length us, event | category | flops | bytes accessed | tf_op | source)
XLA Modules:
  0.0 72.4 jit_solution(15605733140134692467)
XLA Ops:
  0.6 70.2 %shard_map.86 = (bf16[512,384]{1,0:T(8,128)(2,1)S(1)}, bf16[256,768]{1,0:T(8,128)(2,1)S(1)}) custom-call(bf16[512,1536]{1,0:T(8,128)(2,1)} %x_ref.1, f32[1536]{0:T(1024)} %gain_ref.1, bf16[3,384,384]{2,1,0:T(8,128)(2,1)} %bitcast.3, bf16[384,3072]{1,0:T(8,128)(2,1)} %up_ref.1, f32[768]{0:T(1024)} %og_ref.1, s32[1,128]{1,0:T(1,128)} %bitcast.4, s32[1,128]{1,0:T(1,128)} %bitcast.5), custom_call_target="tpu_custom_call" | custom-call | tf_op jit(solution)/shard_map/pallas_call | solution.py:562
  70.9 0.7 %copy.11 = bf16[512,384]{1,0:T(8,128)(2,1)} copy(bf16[512,384]{1,0:T(8,128)(2,1)S(1)} %get-tuple-element.4) | data formatting | bytes 786432
  71.6 0.7 %copy.12 = bf16[256,768]{1,0:T(8,128)(2,1)} copy(bf16[256,768]{1,0:T(8,128)(2,1)S(1)} %get-tuple-element.5) | data formatting | bytes 786432

commit v3 on v2

--- a/solution.py
+++ b/solution.py
@@ -37,9 +37,6 @@
     qbuf,
     kbuf,
     vbuf,
-    obuf,
-    mbuf,
-    lbuf,
     place,
     outrows,
     arrived,
@@ -65,6 +62,7 @@
     all_recv,
     sq_send,
     sq_recv,
+    go,
 ):
     n_seq, n_phase, reach, slot = dims
     tok, d = xbuf.shape
@@ -271,56 +269,63 @@
     tq = min(tok, 256)
     scale = HD ** (-0.5) * math.log2(math.e)
 
-    def attend(dist, h):
+    def scores(h, r, q0, dist, k0, size):
+        s = lax.dot_general(
+            qbuf[h, r, :],
+            kbuf[h, dist, k0 : k0 + size],
+            (((1,), (1,)), ((), ())),
+            preferred_element_type=jnp.float32,
+        )
+        ahead = k0 - dist * tok - q0
+        if ahead + size - 1 > 0 or ahead - (tq - 1) <= -WINDOW:
+            gap = lax.broadcasted_iota(jnp.int32, s.shape, 1) - lax.broadcasted_iota(jnp.int32, s.shape, 0)
+            s = jnp.where((gap <= -ahead) & (gap > -ahead - WINDOW), s, NEG)
+        return s
+
+    def chunks(dist, q0, size=256):
+        out = []
+        for k0 in range(0, tok, size):
+            ahead = k0 - dist * tok - q0
+            if ahead - (tq - 1) <= 0 and ahead + size - 1 > -WINDOW:
+                out.append((dist, k0, size))
+        return out
+
+    def attend(h, dists):
+        tiles = []
         for q0 in range(0, tok, tq):
             r = pl.ds(q0, tq)
-            low = max(0, q0 + dist * tok - WINDOW + 1) // 128 * 128
-            keys = slice(low, tok if dist else q0 + tq)
-            s = lax.dot_general(
-                qbuf[h, r, :],
-                kbuf[dist, keys],
-                (((1,), (1,)), ((), ())),
-                preferred_element_type=jnp.float32,
-            )
-            if dist == 0 or (dist + 1) * tok - 1 >= WINDOW:
-                qi = q0 + lax.broadcasted_iota(jnp.int32, s.shape, 0)
-                kj = lax.broadcasted_iota(jnp.int32, s.shape, 1) + (low - dist * tok)
-                s = jnp.where((kj <= qi) & (kj > qi - WINDOW), s, NEG)
-            top = jnp.max(s, axis=1, keepdims=True)
-            if dist > 0:
-                old = mbuf[h, r, :]
-                top = jnp.maximum(top, old)
-            e = jnp.exp2(s * scale - top * scale)
-            total = jnp.sum(e, axis=1, keepdims=True)
-            o = jnp.dot(e.astype(jnp.bfloat16), vbuf[dist, keys], preferred_element_type=jnp.float32)
-            if dist > 0:
-                fade = jnp.exp2((old - top) * scale)
-                total = total + fade * lbuf[h, r, :]
-                o = o + fade * obuf[h, r, :]
-            mbuf[h, r, :] = top
-            lbuf[h, r, :] = total
-            obuf[h, r, :] = o
-
-    def own_block(h, also=None):
-        if also is not None:
-            pl.when(also)(lambda: own_block(h))
-            return
-        w = jnp.concatenate([wbuf[h, j] for j in range(3)], axis=1)
-        got = jnp.dot(normed[...], w, preferred_element_type=jnp.float32).astype(jnp.bfloat16)
-        qbuf[h] = got[:, :HD]
-        kbuf[0] = got[:, HD : 2 * HD]
-        vbuf[0] = got[:, 2 * HD :]
-        attend(0, h)
-
-    def earlier_block(h, dist, also=True):
+            where = [at for dist in dists for at in chunks(dist, q0)]
+            tiles.append((r, where, [scores(h, r, q0, *at) for at in where]))
+        for r, where, parts in tiles:
+            top = jnp.max(functools.reduce(jnp.maximum, parts), axis=1, keepdims=True)
+            low = top * scale
+            es = [jnp.exp2(s * scale - low) for s in parts]
+            total = jnp.sum(functools.reduce(jnp.add, es), axis=1, keepdims=True)
+            e = jnp.concatenate([e.astype(jnp.bfloat16) for e in es], axis=1)
+            v = jnp.concatenate([vbuf[h, dist, k0 : k0 + size] for dist, k0, size in where], axis=0)
+            o = jnp.dot(e, v, preferred_element_type=jnp.float32)
+            att = (o / total).astype(jnp.bfloat16).astype(jnp.float32)
+            res = xbuf[r, pl.ds(pl.multiple_of(p * width + h * HD, HD), HD)].astype(jnp.float32)
+            bs_ref[r, h * HD : (h + 1) * HD] = (res + att).astype(jnp.bfloat16)
+
+    def store(h, dist, got):
+        start = min(dist, 1) * HD
+        if dist == 0:
+            qbuf[h] = got[:, :HD]
+        kbuf[h, dist] = got[:, HD - start : 2 * HD - start]
+        vbuf[h, dist] = got[:, 2 * HD - start :]
+
+    def project(h, dist, also=True):
         @pl.when((z >= dist) & also)
         def _():
-            w = jnp.concatenate([wbuf[h, j] for j in range(1, 3)], axis=1)
-            rows_in = jnp.concatenate([halo[dist - 1, q] for q in range(n_phase)], axis=1)
-            got = jnp.dot(rows_in, w, preferred_element_type=jnp.float32).astype(jnp.bfloat16)
-            kbuf[dist] = got[:, :HD]
-            vbuf[dist] = got[:, HD:]
-            attend(dist, h)
+            w = jnp.concatenate([wbuf[h, j] for j in range(min(dist, 1), 3)], axis=1)
+            rows_in = (
+                jnp.concatenate([halo[dist - 1, q] for q in range(n_phase)], axis=1)
+                if dist
+                else normed[...]
+            )
+            got = jnp.dot(rows_in, w, preferred_element_type=jnp.float32)
+            store(h, dist, got.astype(jnp.bfloat16))
 
     def split_rows(dist):
         if dist == 0:
@@ -346,29 +351,28 @@
                 split_rows(dist)[0], some_weights(dist, slice(0, rows)), preferred_element_type=jnp.float32
             )
             start = min(dist, 1) * HD
-            got = (got + partial[dist, :, pl.ds(start, got.shape[1])]).astype(jnp.bfloat16)
-            if dist == 0:
-                qbuf[last] = got[:, :HD]
-            kbuf[dist] = got[:, HD - start : 2 * HD - start]
-            vbuf[dist] = got[:, 2 * HD - start :]
-            attend(dist, last)
+            store(last, dist, (got + partial[dist, :, pl.ds(start, got.shape[1])]).astype(jnp.bfloat16))
 
     def close(h):
-        at = slice(h * HD, (h + 1) * HD)
-        res = xbuf[:, pl.ds(pl.multiple_of(p * width + h * HD, HD), HD)].astype(jnp.float32)
-        att = (obuf[h] / lbuf[h]).astype(jnp.bfloat16).astype(jnp.float32)
-        states = (res + att).astype(jnp.bfloat16)
-        bs_ref[:, at] = states
+        for n in range(reach + 1):
+
+            @pl.when(z == n if n < reach else z >= n)
+            def _():
+                attend(h, list(range(n, -1, -1)))
+
+        states = bs_ref[:, h * HD : (h + 1) * HD]
         routed = jnp.dot(place[...], states, preferred_element_type=jnp.float32).astype(jnp.bfloat16)
         for s in range(n_seq):
             outrows[h, s] = routed[s * slot : (s + 1) * slot]
         arrived[h, p, z] = outrows[h, z]
         rows_out(h, False)
 
+    outer = n_seq - 2
+
     def rows_out(h, held):
         for k in range(1, n_seq):
             other = lax.rem(z + k, n_seq)
-            wait = (other > z) & (other >= n_seq - 2)
+            wait = (z < outer) & (other >= outer)
             send(
                 outrows.at[h, other],
                 arrived.at[h, p, z],
@@ -378,8 +382,6 @@
                 wait if held else jnp.logical_not(wait),
             )
 
-    outer = n_seq - 2
-
     def rows_in(h, j, cond):
         if j == 0:
             landed(arrived.at[h, p, pl.ds(0, outer)], row_recv.at[h, 0], cond & (z >= outer))
@@ -388,9 +390,8 @@
             src = outer + j - 1
             landed(arrived.at[h, p, src], row_recv.at[h, j], cond & (z != src))
 
-    def spread(h, j, cond, waited=False):
-        if not waited:
-            rows_in(h, j, cond)
+    def spread(h, j, cond):
+        rows_in(h, j, cond)
         piece = arrived.at[h, p, pl.ds(0, outer) if j == 0 else pl.ds(outer + j - 1, 1)]
         group = 1 + j // 2 if h == last else 0
         for k in range(1, n_phase):
@@ -417,78 +418,82 @@
     for t in range(3, n_seq):
         relay(0, t, RIGHTWARD)
     finish(0)
-    own_block(0)
+    project(0, 0)
     relay(1, 1, RIGHTWARD, (z > 1) & (z < n_seq - 1))
     relay(1, 2, RIGHTWARD, z < n_seq - 1)
     issue_own(2, RIGHTWARD, z > 1)
     for dist in range(1, reach):
         halo_wait(dist)
-        earlier_block(0, dist)
+        project(0, dist)
     relay(1, 1, RIGHTWARD, final)
     relay(1, 2, RIGHTWARD, final)
     halo_pass(reach, final)
     for t in range(3, n_seq):
         relay(1, t, RIGHTWARD)
     finish(1)
-    own_block(1)
+    project(1, 0)
     relay(2, 1, RIGHTWARD, (z > 1) & (z < n_seq - 1))
     for dist in range(1, reach):
-        earlier_block(1, dist)
+        project(1, dist)
     halo_pass(reach, z < n_seq - 1)
     relay(2, 1, RIGHTWARD, final)
     relay(2, 2, RIGHTWARD, z < n_seq - 1)
     inner = z < n_seq - 1
     finish(last, False, inner)
     finish(last, True, inner)
-    own_block(last, inner)
+    project(last, 0, inner)
     for dist in range(1, reach):
-        earlier_block(last, dist, inner)
+        project(last, dist, inner)
     halo_wait(reach)
     outside = z < outer
     for h in range(last):
-        earlier_block(h, reach)
-        if h == last - 1:
-            for t in range(3, n_seq):
-                relay(last, t, RIGHTWARD, c == 1)
+        project(h, reach)
         close(h)
         if h == 0:
             relay(last, 2, RIGHTWARD, final)
+
+            @pl.when(final)
+            def _():
+                for far in range(outer):
+                    pl.semaphore_signal(go, inc=1, device_id={"seq": far}, device_id_type=MESH)
+
+    for t in range(3, n_seq):
+        relay(last, t, RIGHTWARD, c == 1)
     for h in range(last):
         spread(h, 2, final)
     finish(last, False, final)
-    for dist in range(reach):
-        project_early(dist, final)
+    project_early(0, final)
     for t in range(3, n_seq):
         relay(last, t, RIGHTWARD, c == 0)
-    project_early(reach, final)
+    for dist in range(1, reach + 1):
+        project_early(dist, final)
+    for h in range(last):
+        spread(h, 1, final)
     finish(last, True, final)
     for dist in range(reach + 1):
         project_late(dist, final)
-        if dist == 0:
-            for h in range(last):
-                spread(h, 1, final)
     for h in range(last):
         spread(h, 1, z == outer)
-    rows_in(0, 2, z == outer)
-    for h in range(last):
-        pl.when(z == outer)(lambda h=h: rows_out(h, True))
-    earlier_block(last, reach, inner)
+    project(last, reach, inner)
     close(last)
-    pl.when(z == outer)(lambda: rows_out(last, True))
     spread(last, 1, z == outer)
     spread(last, 2, final)
     for h in range(heads):
+        spread(h, 0, final)
+    for h in range(heads):
         spread(h, 0, outside)
-    rows_in(0, 2, outside)
-    for h in range(heads):
-        pl.when(outside)(lambda h=h: rows_out(h, True))
-    spread(0, 1, outside)
-    spread(0, 2, inner, waited=True)
-    for h in range(1, last):
+
+    @pl.when(outside)
+    def _():
+        pl.semaphore_wait(go, 1)
+        for h in range(heads):
+            rows_out(h, True)
+
+    for h in range(last):
         spread(h, 1, outside)
         spread(h, 2, inner)
     for h in range(heads):
-        spread(h, 0, z >= outer)
+        spread(h, 0, z == outer)
     spread(last, 1, z != outer)
     own_up.wait()
     landed(upbuf.at[pl.ds(0, n_phase - 1), up_half], upp_recv)
@@ -518,9 +523,9 @@
         sq = jnp.sum(projected * projected, axis=1, keepdims=True)
         return jnp.broadcast_to(sq, (r.stop - r.start, 128))
 
+    spread(last, 2, inner)
     landed(arrived.at[last, pl.ds(0, n_phase - 1), pl.ds(0, n_seq - 1)], all_recv.at[1])
     sq_top = complete(0)
-    spread(last, 2, inner)
     landed(arrived.at[last, pl.ds(0, n_phase - 1), pl.ds(0, 1)], all_recv.at[2])
     sq_all = jnp.concatenate([sq_top, complete(1)], axis=0)
     sqbuf[p] = sq_all.T[0:8, :]
@@ -544,6 +549,17 @@
     sent(outrows.at[:, pl.ds(0, n_seq - 1)], row_send)
     sent(arrived.at[:, pl.ds(0, n_phase - 1)], all_send)
     sent(sqbuf.at[pl.ds(0, n_phase - 1)], sq_send)
+
+
+def flush_kernel(a_ref, b_ref, a_out, b_out, sems):
+    copies = [
+        pltpu.make_async_copy(a_ref, a_out, sems.at[0]),
+        pltpu.make_async_copy(b_ref, b_out, sems.at[1]),
+    ]
+    for copy in copies:
+        copy.start()
+    for copy in copies:
+        copy.wait()
 
 
 def fused(n_seq, n_phase, byte_embed, in_gain, w_qkv, w_up, out_gain, bounds, owner):
@@ -578,11 +594,8 @@
             pltpu.VMEM((heads, 3, n_seq * rows, HD), bf),
             pltpu.VMEM((n_phase, w_up.shape[0], cols), bf),
             pltpu.VMEM((heads, tok, HD), bf),
-            pltpu.VMEM((reach + 1, tok, HD), bf),
-            pltpu.VMEM((reach + 1, tok, HD), bf),
-            pltpu.VMEM((heads, tok, HD), f32),
-            pltpu.VMEM((heads, tok, 1), f32),
-            pltpu.VMEM((heads, tok, 1), f32),
+            pltpu.VMEM((heads, reach + 1, tok, HD), bf),
+            pltpu.VMEM((heads, reach + 1, tok, HD), bf),
             pltpu.VMEM((n_seq * slot, tok), bf),
             pltpu.VMEM((heads, n_seq, slot, HD), bf),
             pltpu.VMEM((heads, n_phase, n_seq, slot, HD), bf),
@@ -608,6 +621,7 @@
             dma((3,)),
             dma(()),
             dma(()),
+            pltpu.SemaphoreType.REGULAR,
         ],
         compiler_params=pltpu.CompilerParams(
             collective_id=0, has_side_effects=True, vmem_limit_bytes=48 * 1024 * 1024
@@ -621,7 +635,17 @@
         in_hbm(bounds.reshape(1, crows)),
         in_hbm(owner.reshape(1, crows)),
     )
-    return states, stretch
+    return pl.pallas_call(
+        flush_kernel,
+        out_shape=(
+            jax.ShapeDtypeStruct(states.shape, bf),
+            jax.ShapeDtypeStruct(stretch.shape, bf),
+        ),
+        in_specs=[vmem] * 2,
+        out_specs=(hbm, hbm),
+        scratch_shapes=[dma((2,))],
+        compiler_params=pltpu.CompilerParams(vmem_limit_bytes=4 * 1024 * 1024),
+    )(states, stretch)
 
 
 def passed_along(value, axis, by):

time: 72.5 us -> 69.4 us (0.957)
  Pallas kernels: 70.2 us -> 68.5 us
  local copies, waits for them, and re-layouts: 1.49 us -> 0 us
    pallas_call x1, Pallas kernels: 70.2 us -> 67.6 us  [fused(): pl.pallas_call(functools.partial(fused_kernel, (n_seq, n_phase, reach, sl...]
    unnamed x2 -> x0, local copies, waits for them, and re-layouts: 1.49 us -> none
    pallas_call x0 -> x1, Pallas kernels: none -> 0.89 us  [fused(): pl.pallas_call(flush_kernel, out_shape=(jax.ShapeDtypeStruct(states.shape...]
where the time goes in v3:
time: 69.4 us; the launch traced here: 69.3 us
  Pallas kernels  68.5 us (99%)
  between operations  0.8 us (1%)
    pallas_call x1, Pallas kernels, fused(): pl.pallas_call(functools.partial(fused_kernel, (n_seq, n_phase, reach, sl...  67.6 us

profile of v3, /device:TPU:0, one launch (start us, length us, event | category | flops | bytes accessed | tf_op | source)
XLA Modules:
  0.0 69.3 jit_solution(9913644689491019)
XLA Ops:
  0.6 67.6 %shard_map.86 = (bf16[512,384]{1,0:T(8,128)(2,1)S(1)}, bf16[256,768]{1,0:T(8,128)(2,1)S(1)}) custom-call(bf16[512,1536]{1,0:T(8,128)(2,1)} %x_ref.1, f32[1536]{0:T(1024)} %gain_ref.1, bf16[3,384,384]{2,1,0:T(8,128)(2,1)} %bitcast.3, bf16[384,3072]{1,0:T(8,128)(2,1)} %up_ref.1, f32[768]{0:T(1024)} %og_ref.1, s32[1,128]{1,0:T(1,128)} %bitcast.4, s32[1,128]{1,0:T(1,128)} %bitcast.5), custom_call_target="tpu_custom_call" | custom-call | tf_op jit(solution)/shard_map/pallas_call | solution.py:578
  68.2 0.9 %shard_map.87 = (bf16[512,384]{1,0:T(8,128)(2,1)}, bf16[256,768]{1,0:T(8,128)(2,1)}) custom-call(bf16[512,384]{1,0:T(8,128)(2,1)S(1)} %get-tuple-element.4.a_ref, bf16[256,768]{1,0:T(8,128)(2,1)S(1)} %get-tuple-element.5.b_ref), custom_call_target="tpu_custom_call" | custom-call | tf_op jit(solution)/shard_map/pallas_call | solution.py:638

commit v4 on v3

--- a/solution.py
+++ b/solution.py
@@ -177,42 +177,42 @@
 
     across = {1: {"phase": p + 1 - 2 * lax.rem(p, 2)}, 2: {"phase": lax.rem(p + 2, n_phase)}}
     spots = {k: v["phase"] for k, v in across.items()}
-    mine = {}
-
-    def halo_start(dist, cond):
-        own_part = normed.at[:, pl.ds(pl.multiple_of(p * width, 128), width)]
-        src = own_part if dist == 1 else halo.at[dist - 2, p]
-        mine[dist] = send(src, halo.at[dist - 1, p], h_send.at[dist - 1], h_recv.at[dist - 1], right, cond)
-
-    gathers = {}
-
-    def halo_spread(dist):
+    parts = [pl.ds(i * (tok // 2), tok // 2) for i in range(2)]
+    mine, gathers = {}, {}
+
+    def halo_start(dist, i, cond):
+        if dist == 1:
+            src = normed.at[parts[i], pl.ds(pl.multiple_of(p * width, 128), width)]
+        else:
+            src = halo.at[dist - 2, p, parts[i]]
+        mine[dist, i] = send(
+            src, halo.at[dist - 1, p, parts[i]], h_send.at[dist - 1], h_recv.at[dist - 1, i], right, cond
+        )
+
+    def halo_spread(dist, i):
         there = z >= dist
-        pl.when(there)(mine[dist].wait_recv)
+        pl.when(there)(mine[dist, i].wait_recv)
         if dist < reach:
-            halo_start(dist + 1, there & has_right)
+            halo_start(dist + 1, i, there & has_right)
+        piece = halo.at[dist - 1, p, parts[i]]
         for k in (1, 2):
-            piece = halo.at[dist - 1, p]
-            gathers[dist, k] = send(
-                piece, piece, g_send.at[dist - 1], g_recv.at[dist - 1, k - 1], across[k], there
+            gathers[dist, i, k] = send(
+                piece, piece, g_send.at[dist - 1], g_recv.at[dist - 1, 2 * i + k - 1], across[k], there
             )
 
-    def halo_pass(dist, also=None):
-        there = z >= dist
-        if also is not None:
-            there = there & also
-        for k in (1, 2):
-            pl.when(there)(gathers[dist, k].wait_recv)
-            part = pl.ds((k - 1) * (tok // 2), tok // 2)
-            piece = halo.at[dist - 1, spots[k], part]
-            gathers[dist, 2 + k] = send(
-                piece, piece, g_send.at[dist - 1], g_recv.at[dist - 1, 2], across[3 - k], there
-            )
+    def halo_pass(dist, i, also=True):
+        there = (z >= dist) & also
+        k = i + 1
+        pl.when(there)(gathers[dist, i, k].wait_recv)
+        piece = halo.at[dist - 1, spots[k], parts[i]]
+        send(piece, piece, g_send.at[dist - 1], g_recv.at[dist - 1, 4], across[3 - k], there)
 
     def halo_wait(dist):
         @pl.when(z >= dist)
         def _():
-            landed(halo.at[dist - 1, 0], g_recv.at[dist - 1, 2])
+            gathers[dist, 0, 2].wait_recv()
+            gathers[dist, 1, 1].wait_recv()
+            landed(halo.at[dist - 1, 0], g_recv.at[dist - 1, 4])
 
     own_w[0].wait()
     issue_own(0, RIGHTWARD)
@@ -222,10 +222,19 @@
         issue_own(h, LEFTWARD)
     up_rows = up_ref.shape[0] // 2
     up_half = pl.ds(pl.multiple_of(c * up_rows, up_rows), up_rows)
-    for k in range(1, n_phase):
-        other = lax.rem(p + k, n_phase)
+
+    def up_out(k):
+        other = spots[k] if k < 3 else n_phase - 1 - p
         part = pl.ds(pl.multiple_of(other * cols, 128), cols)
-        send(up_ref.at[up_half, part], upbuf.at[p, up_half], up_send, up_recv, {"phase": other})
+        group = 0 if k < 3 else 1
+        send(up_ref.at[up_half, part], upbuf.at[p, up_half], up_send, up_recv.at[group], {"phase": other})
+
+    def up_in(k):
+        piece = upbuf.at[spots[k] if k < 3 else n_phase - 1 - p, up_half]
+        send(piece, piece, upp_send, upp_recv, twin_core)
+
+    for k in (1, 2):
+        up_out(k)
 
     own_x.wait()
     small[0].wait()
@@ -239,7 +248,8 @@
         scale = lax.rsqrt(jnp.mean(xx * xx, axis=1, keepdims=True) + 1e-05)
         normed[r, :] = (xx * scale * gain[...]).astype(jnp.bfloat16)
 
-    halo_start(1, has_right)
+    for i in range(2):
+        halo_start(1, i, has_right)
     first, second, final = z == 0, z == 1, z == n_seq - 1
     for h in range(1, heads):
         issue_own(h, RIGHTWARD, first)
@@ -353,13 +363,14 @@
             start = min(dist, 1) * HD
             store(last, dist, (got + partial[dist, :, pl.ds(start, got.shape[1])]).astype(jnp.bfloat16))
 
-    def close(h):
+    def heed(h):
         for n in range(reach + 1):
 
             @pl.when(z == n if n < reach else z >= n)
             def _():
                 attend(h, list(range(n, -1, -1)))
 
+    def hand_over(h):
         states = bs_ref[:, h * HD : (h + 1) * HD]
         routed = jnp.dot(place[...], states, preferred_element_type=jnp.float32).astype(jnp.bfloat16)
         for s in range(n_seq):
@@ -368,6 +379,10 @@
         rows_out(h, False)
 
     outer = n_seq - 2
+
+    def close(h):
+        heed(h)
+        hand_over(h)
 
     def rows_out(h, held):
         for k in range(1, n_seq):
@@ -397,76 +412,91 @@
         for k in range(1, n_phase):
             send(piece, piece, all_send, all_recv.at[group], {"phase": lax.rem(p + k, n_phase)}, cond)
 
-    for h in range(1, heads):
-        relay(h, 1, LEFTWARD)
-    halo_spread(1)
-    landed(upbuf.at[pl.ds(0, n_phase - 1), up_half], up_recv)
-    for k in range(1, n_phase):
-        piece = upbuf.at[lax.rem(p + n_phase - k, n_phase), up_half]
-        send(piece, piece, upp_send, upp_recv, twin_core)
+    relay(1, 1, LEFTWARD)
+    halo_spread(1, 0)
+    relay(2, 1, LEFTWARD)
+    landed(upbuf.at[pl.ds(0, 2), up_half], up_recv.at[0])
+    for k in (1, 2):
+        up_in(k)
+    halo_spread(1, 1)
     for h in range(1, heads):
         issue_own(h, RIGHTWARD, second)
         relay(h, 1, RIGHTWARD, second)
+    halo_pass(1, 0)
     relay(0, 2, RIGHTWARD)
     issue_own(1, RIGHTWARD, z > 1)
+    halo_pass(1, 1)
     for t in range(2, n_seq):
         for h in range(heads):
             relay(h, t, LEFTWARD)
     for dist in range(2, reach + 1):
-        halo_pass(dist - 1)
-        halo_spread(dist)
+        for i in range(2):
+            halo_spread(dist, i)
     for t in range(3, n_seq):
         relay(0, t, RIGHTWARD)
+    inner, outside = z < n_seq - 1, z < outer
+    halo_pass(reach, 0, final)
     finish(0)
     project(0, 0)
-    relay(1, 1, RIGHTWARD, (z > 1) & (z < n_seq - 1))
-    relay(1, 2, RIGHTWARD, z < n_seq - 1)
+    relay(1, 1, RIGHTWARD, (z > 1) & inner)
+    halo_pass(reach, 0, inner)
+    relay(1, 2, RIGHTWARD, inner)
     issue_own(2, RIGHTWARD, z > 1)
     for dist in range(1, reach):
         halo_wait(dist)
         project(0, dist)
+    halo_pass(reach, 1)
     relay(1, 1, RIGHTWARD, final)
     relay(1, 2, RIGHTWARD, final)
-    halo_pass(reach, final)
+    up_out(3)
     for t in range(3, n_seq):
         relay(1, t, RIGHTWARD)
+
+    @pl.when(final)
+    def _():
+        halo_wait(reach)
+        project(0, reach)
+        heed(0)
+
     finish(1)
     project(1, 0)
-    relay(2, 1, RIGHTWARD, (z > 1) & (z < n_seq - 1))
+    relay(2, 1, RIGHTWARD, (z > 1) & inner)
     for dist in range(1, reach):
         project(1, dist)
-    halo_pass(reach, z < n_seq - 1)
     relay(2, 1, RIGHTWARD, final)
-    relay(2, 2, RIGHTWARD, z < n_seq - 1)
-    inner = z < n_seq - 1
+    relay(2, 2, RIGHTWARD, inner)
     finish(last, False, inner)
     finish(last, True, inner)
     project(last, 0, inner)
     for dist in range(1, reach):
         project(last, dist, inner)
-    halo_wait(reach)
-    outside = z < outer
-    for h in range(last):
+
+    @pl.when(inner)
+    def _():
+        halo_wait(reach)
+        project(0, reach)
+        heed(0)
+
+    hand_over(0)
+    for h in range(1, last):
         project(h, reach)
         close(h)
-        if h == 0:
-            relay(last, 2, RIGHTWARD, final)
-
-            @pl.when(final)
-            def _():
-                for far in range(outer):
-                    pl.semaphore_signal(go, inc=1, device_id={"seq": far}, device_id_type=MESH)
-
+
+    @pl.when(final)
+    def _():
+        for far in range(outer):
+            pl.semaphore_signal(go, inc=1, device_id={"seq": far}, device_id_type=MESH)
+
+    relay(last, 2, RIGHTWARD, final)
     for t in range(3, n_seq):
         relay(last, t, RIGHTWARD, c == 1)
     for h in range(last):
         spread(h, 2, final)
     finish(last, False, final)
-    project_early(0, final)
+    for dist in range(reach + 1):
+        project_early(dist, final)
     for t in range(3, n_seq):
         relay(last, t, RIGHTWARD, c == 0)
-    for dist in range(1, reach + 1):
-        project_early(dist, final)
     for h in range(last):
         spread(h, 1, final)
     finish(last, True, final)
@@ -480,6 +510,8 @@
     spread(last, 2, final)
     for h in range(heads):
         spread(h, 0, final)
+    landed(upbuf.at[0, up_half], up_recv.at[1])
+    up_in(3)
     for h in range(heads):
         spread(h, 0, outside)
 
@@ -608,13 +640,13 @@
             dma(()),
             dma((heads + 1,)),
             dma(()),
-            dma(()),
+            dma((2,)),
             dma(()),
             dma(()),
             dma((reach,)),
+            dma((reach, 2)),
             dma((reach,)),
-            dma((reach,)),
-            dma((reach, 3)),
+            dma((reach, 5)),
             dma(()),
             dma((heads, 3)),
             dma(()),

time: 69.4 us -> 68.2 us (0.983)
  Pallas kernels: 68.5 us -> 67.2 us
    pallas_call x1, Pallas kernels: 67.6 us -> 66.3 us  [fused(): pl.pallas_call(functools.partial(fused_kernel, (n_seq, n_phase, reach, sl...]
where the time goes in v4:
time: 68.2 us; the launch traced here: 68 us
  Pallas kernels  67.2 us (99%)
  between operations  0.8 us (1%)
    pallas_call x1, Pallas kernels, fused(): pl.pallas_call(functools.partial(fused_kernel, (n_seq, n_phase, reach, sl...  66.3 us

profile of v4, /device:TPU:0, one launch (start us, length us, event | category | flops | bytes accessed | tf_op | source)
XLA Modules:
  0.0 68.0 jit_solution(2335599018349774289)
XLA Ops:
  0.6 66.3 %shard_map.86 = (bf16[512,384]{1,0:T(8,128)(2,1)S(1)}, bf16[256,768]{1,0:T(8,128)(2,1)S(1)}) custom-call(bf16[512,1536]{1,0:T(8,128)(2,1)} %x_ref.1, f32[1536]{0:T(1024)} %gain_ref.1, bf16[3,384,384]{2,1,0:T(8,128)(2,1)} %bitcast.3, bf16[384,3072]{1,0:T(8,128)(2,1)} %up_ref.1, f32[768]{0:T(1024)} %og_ref.1, s32[1,128]{1,0:T(1,128)} %bitcast.4, s32[1,128]{1,0:T(1,128)} %bitcast.5), custom_call_target="tpu_custom_call" | custom-call | tf_op jit(solution)/shard_map/pallas_call | solution.py:610
  67.0 0.9 %shard_map.87 = (bf16[512,384]{1,0:T(8,128)(2,1)}, bf16[256,768]{1,0:T(8,128)(2,1)}) custom-call(bf16[512,384]{1,0:T(8,128)(2,1)S(1)} %get-tuple-element.4.a_ref, bf16[256,768]{1,0:T(8,128)(2,1)S(1)} %get-tuple-element.5.b_ref), custom_call_target="tpu_custom_call" | custom-call | tf_op jit(solution)/shard_map/pallas_call | solution.py:670

commit v5 on v4

--- a/solution.py
+++ b/solution.py
@@ -82,7 +82,7 @@
     for i, (src, dst) in enumerate(
         ((gain_ref, gain.at[0]), (bounds_ref, bnd), (owner_ref, own), (og_ref, og.at[0]))
     ):
-        small.append(pltpu.make_async_copy(src, dst, loc_sem.at[2 + heads + i]))
+        small.append(pltpu.make_async_copy(src, dst, loc_sem.at[3 + i]))
         small[i].start()
 
     twin_core = {"dp": 1 - c}
@@ -95,20 +95,6 @@
     for peer in peers:
         pl.semaphore_signal(barrier, inc=1, device_id=peer, device_id_type=MESH)
 
-    own_w = []
-    for h in range(heads):
-        own_w.append(
-            pltpu.make_async_copy(
-                w_ref.at[:, :, pl.ds(h * HD, HD)],
-                wbuf.at[h, :, pl.ds(pl.multiple_of(z * rows, rows), rows), :],
-                loc_sem.at[2 + h],
-            )
-        )
-        own_w[h].start()
-    own_up = pltpu.make_async_copy(
-        up_ref.at[:, pl.ds(pl.multiple_of(p * cols, 128), cols)], upbuf.at[p], loc_sem.at[1]
-    )
-    own_up.start()
     pl.semaphore_wait(barrier, len(peers))
 
     def when(cond, action):
@@ -146,7 +132,7 @@
         return t - 1 if way == LEFTWARD else n_seq - t - 1
 
     def issue_own(h, way, also=None):
-        src = chunk(h, z)
+        src = w_ref.at[:, pl.ds(pl.multiple_of(c * half, half), half), pl.ds(h * HD, HD)]
         peer, cond, sign = ways[way]
         cond = cond if also is None else cond & also
         send(src, chunk(h, z), w_send, w_recv.at[h, slot_of(1, way)], peer, cond)
@@ -177,6 +163,7 @@
 
     across = {1: {"phase": p + 1 - 2 * lax.rem(p, 2)}, 2: {"phase": lax.rem(p + 2, n_phase)}}
     spots = {k: v["phase"] for k, v in across.items()}
+    partners = (n_phase - 1 - p, spots[1], spots[2])
     parts = [pl.ds(i * (tok // 2), tok // 2) for i in range(2)]
     mine, gathers = {}, {}
 
@@ -196,8 +183,9 @@
             halo_start(dist + 1, i, there & has_right)
         piece = halo.at[dist - 1, p, parts[i]]
         for k in (1, 2):
+            group = i if k == i + 1 else 2
             gathers[dist, i, k] = send(
-                piece, piece, g_send.at[dist - 1], g_recv.at[dist - 1, 2 * i + k - 1], across[k], there
+                piece, piece, g_send.at[dist - 1], g_recv.at[dist - 1, group], across[k], there
             )
 
     def halo_pass(dist, i, also=True):
@@ -205,29 +193,25 @@
         k = i + 1
         pl.when(there)(gathers[dist, i, k].wait_recv)
         piece = halo.at[dist - 1, spots[k], parts[i]]
-        send(piece, piece, g_send.at[dist - 1], g_recv.at[dist - 1, 4], across[3 - k], there)
+        send(piece, piece, g_send.at[dist - 1], g_recv.at[dist - 1, 2], across[3 - k], there)
 
     def halo_wait(dist):
         @pl.when(z >= dist)
         def _():
-            gathers[dist, 0, 2].wait_recv()
-            gathers[dist, 1, 1].wait_recv()
-            landed(halo.at[dist - 1, 0], g_recv.at[dist - 1, 4])
-
-    own_w[0].wait()
+            landed(halo.at[dist - 1, pl.ds(0, 2)], g_recv.at[dist - 1, 2])
+
     issue_own(0, RIGHTWARD)
-    issue_own(0, LEFTWARD)
-    for h in range(1, heads):
-        own_w[h].wait()
+    for h in range(heads):
         issue_own(h, LEFTWARD)
     up_rows = up_ref.shape[0] // 2
     up_half = pl.ds(pl.multiple_of(c * up_rows, up_rows), up_rows)
 
-    def up_out(k):
+    def up_out(k, also=None):
         other = spots[k] if k < 3 else n_phase - 1 - p
         part = pl.ds(pl.multiple_of(other * cols, 128), cols)
         group = 0 if k < 3 else 1
-        send(up_ref.at[up_half, part], upbuf.at[p, up_half], up_send, up_recv.at[group], {"phase": other})
+        dst = upbuf.at[p, up_half]
+        send(up_ref.at[up_half, part], dst, up_send, up_recv.at[group], {"phase": other}, also)
 
     def up_in(k):
         piece = upbuf.at[spots[k] if k < 3 else n_phase - 1 - p, up_half]
@@ -235,6 +219,17 @@
 
     for k in (1, 2):
         up_out(k)
+    mine_w = wbuf.at[:, :, pl.ds(pl.multiple_of(z * rows, rows), rows), :]
+    for h in range(heads):
+        pltpu.make_async_copy(
+            w_ref.at[:, :, pl.ds(h * HD, HD)],
+            wbuf.at[h, :, pl.ds(pl.multiple_of(z * rows, rows), rows), :],
+            loc_sem.at[2],
+        ).start()
+    own_up = pltpu.make_async_copy(
+        up_ref.at[:, pl.ds(pl.multiple_of(p * cols, 128), cols)], upbuf.at[p], loc_sem.at[1]
+    )
+    own_up.start()
 
     own_x.wait()
     small[0].wait()
@@ -260,6 +255,7 @@
 
     relay(0, 1, RIGHTWARD)
     relay(0, 1, LEFTWARD)
+    pltpu.make_async_copy(mine_w, mine_w, loc_sem.at[2]).wait()
     for copy in small[1:]:
         copy.wait()
     local = column(bnd)[:, 0:1] - (z * tok).astype(jnp.float32)
@@ -384,6 +380,12 @@
         heed(h)
         hand_over(h)
 
+    def release(cond):
+        @pl.when(cond)
+        def _():
+            for far in range(outer):
+                pl.semaphore_signal(go, inc=1, device_id={"seq": far}, device_id_type=MESH)
+
     def rows_out(h, held):
         for k in range(1, n_seq):
             other = lax.rem(z + k, n_seq)
@@ -409,8 +411,8 @@
         rows_in(h, j, cond)
         piece = arrived.at[h, p, pl.ds(0, outer) if j == 0 else pl.ds(outer + j - 1, 1)]
         group = 1 + j // 2 if h == last else 0
-        for k in range(1, n_phase):
-            send(piece, piece, all_send, all_recv.at[group], {"phase": lax.rem(p + k, n_phase)}, cond)
+        for other in partners:
+            send(piece, piece, all_send, all_recv.at[group], {"phase": other}, cond)
 
     relay(1, 1, LEFTWARD)
     halo_spread(1, 0)
@@ -448,7 +450,7 @@
     halo_pass(reach, 1)
     relay(1, 1, RIGHTWARD, final)
     relay(1, 2, RIGHTWARD, final)
-    up_out(3)
+    up_out(3, inner)
     for t in range(3, n_seq):
         relay(1, t, RIGHTWARD)
 
@@ -458,6 +460,7 @@
         project(0, reach)
         heed(0)
 
+    up_out(3, final)
     finish(1)
     project(1, 0)
     relay(2, 1, RIGHTWARD, (z > 1) & inner)
@@ -481,13 +484,8 @@
     for h in range(1, last):
         project(h, reach)
         close(h)
-
-    @pl.when(final)
-    def _():
-        for far in range(outer):
-            pl.semaphore_signal(go, inc=1, device_id={"seq": far}, device_id_type=MESH)
-
     relay(last, 2, RIGHTWARD, final)
+    release(final)
     for t in range(3, n_seq):
         relay(last, t, RIGHTWARD, c == 1)
     for h in range(last):
@@ -497,8 +495,7 @@
         project_early(dist, final)
     for t in range(3, n_seq):
         relay(last, t, RIGHTWARD, c == 0)
-    for h in range(last):
-        spread(h, 1, final)
+    spread(0, 1, final)
     finish(last, True, final)
     for dist in range(reach + 1):
         project_late(dist, final)
@@ -508,6 +505,8 @@
     close(last)
     spread(last, 1, z == outer)
     spread(last, 2, final)
+    for h in range(1, last):
+        spread(h, 1, final)
     for h in range(heads):
         spread(h, 0, final)
     landed(upbuf.at[0, up_half], up_recv.at[1])
@@ -527,6 +526,7 @@
     for h in range(heads):
         spread(h, 0, z == outer)
     spread(last, 1, z != outer)
+    spread(last, 2, z == outer)
     own_up.wait()
     landed(upbuf.at[pl.ds(0, n_phase - 1), up_half], upp_recv)
     landed(arrived.at[pl.ds(0, last), pl.ds(0, n_phase - 1)], all_recv.at[0])
@@ -555,14 +555,14 @@
         sq = jnp.sum(projected * projected, axis=1, keepdims=True)
         return jnp.broadcast_to(sq, (r.stop - r.start, 128))
 
-    spread(last, 2, inner)
+    spread(last, 2, outside)
     landed(arrived.at[last, pl.ds(0, n_phase - 1), pl.ds(0, n_seq - 1)], all_recv.at[1])
     sq_top = complete(0)
     landed(arrived.at[last, pl.ds(0, n_phase - 1), pl.ds(0, 1)], all_recv.at[2])
     sq_all = jnp.concatenate([sq_top, complete(1)], axis=0)
     sqbuf[p] = sq_all.T[0:8, :]
-    for k in range(1, n_phase):
-        send(sqbuf.at[p], sqbuf.at[p], sq_send, sq_recv, {"phase": lax.rem(p + k, n_phase)})
+    for other in partners:
+        send(sqbuf.at[p], sqbuf.at[p], sq_send, sq_recv, {"phase": other})
     landed(sqbuf.at[pl.ds(0, n_phase - 1)], sq_recv)
     all_sq = sqbuf[0]
     for k in range(1, n_phase):
@@ -634,7 +634,7 @@
             pltpu.VMEM((n_phase, n_seq * slot, cols), f32),
             pltpu.VMEM((reach + 1, tok, 3 * HD), f32),
             pltpu.VMEM((n_phase, 8, n_seq * slot), f32),
-            dma((6 + heads,)),
+            dma((7,)),
             dma(()),
             dma((heads, n_seq - 1)),
             dma(()),
@@ -646,7 +646,7 @@
             dma((reach,)),
             dma((reach, 2)),
             dma((reach,)),
-            dma((reach, 5)),
+            dma((reach, 3)),
             dma(()),
             dma((heads, 3)),
             dma(()),

time: 68.2 us -> 67.8 us (level)
  no operation moved by 1% of the time
where the time goes in v5:
time: 67.8 us; the launch traced here: 67.7 us
  Pallas kernels  66.9 us (99%)
  between operations  0.8 us (1%)
    pallas_call x1, Pallas kernels, fused(): pl.pallas_call(functools.partial(fused_kernel, (n_seq, n_phase, reach, sl...  66 us

profile of v5, /device:TPU:0, one launch (start us, length us, event | category | flops | bytes accessed | tf_op | source)
XLA Modules:
  0.0 67.7 jit_solution(8724682230849652032)
XLA Ops:
  0.6 66.0 %shard_map.86 = (bf16[512,384]{1,0:T(8,128)(2,1)S(1)}, bf16[256,768]{1,0:T(8,128)(2,1)S(1)}) custom-call(bf16[512,1536]{1,0:T(8,128)(2,1)} %x_ref.1, f32[1536]{0:T(1024)} %gain_ref.1, bf16[3,384,384]{2,1,0:T(8,128)(2,1)} %bitcast.3, bf16[384,3072]{1,0:T(8,128)(2,1)} %up_ref.1, f32[768]{0:T(1024)} %og_ref.1, s32[1,128]{1,0:T(1,128)} %bitcast.4, s32[1,128]{1,0:T(1,128)} %bitcast.5), custom_call_target="tpu_custom_call" | custom-call | tf_op jit(solution)/shard_map/pallas_call | solution.py:610
  66.6 0.9 %shard_map.87 = (bf16[512,384]{1,0:T(8,128)(2,1)}, bf16[256,768]{1,0:T(8,128)(2,1)}) custom-call(bf16[512,384]{1,0:T(8,128)(2,1)S(1)} %get-tuple-element.4.a_ref, bf16[256,768]{1,0:T(8,128)(2,1)S(1)} %get-tuple-element.5.b_ref), custom_call_target="tpu_custom_call" | custom-call | tf_op jit(solution)/shard_map/pallas_call | solution.py:670

commit v6 on v5

--- a/solution.py
+++ b/solution.py
@@ -94,8 +94,16 @@
     barrier = pltpu.get_barrier_semaphore()
     for peer in peers:
         pl.semaphore_signal(barrier, inc=1, device_id=peer, device_id_type=MESH)
-
-    pl.semaphore_wait(barrier, len(peers))
+    edge = (z == 0) | (z == n_seq - 1)
+
+    @pl.when(edge)
+    def _():
+        for k in range(1, n_phase):
+            other = {"seq": n_seq - 1 - z, "phase": lax.rem(p + k, n_phase)}
+            pl.semaphore_signal(barrier, inc=1, device_id=other, device_id_type=MESH)
+
+
+    pl.semaphore_wait(barrier, len(peers) + jnp.where(edge, n_phase - 1, 0))
 
     def when(cond, action):
         if cond is None:
@@ -398,6 +406,16 @@
                 {"seq": other},
                 wait if held else jnp.logical_not(wait),
             )
+            if h == last and k == 1 and not held:
+                for far in partners:
+                    send(
+                        outrows.at[h, 0],
+                        arrived.at[h, p, n_seq - 1],
+                        row_send,
+                        all_recv.at[2],
+                        {"seq": 0, "phase": far},
+                        final,
+                    )
 
     def rows_in(h, j, cond):
         if j == 0:
@@ -412,7 +430,7 @@
         piece = arrived.at[h, p, pl.ds(0, outer) if j == 0 else pl.ds(outer + j - 1, 1)]
         group = 1 + j // 2 if h == last else 0
         for other in partners:
-            send(piece, piece, all_send, all_recv.at[group], {"phase": other}, cond)
+            send(piece, piece, all_send.at[group], all_recv.at[group], {"phase": other}, cond)
 
     relay(1, 1, LEFTWARD)
     halo_spread(1, 0)
@@ -555,12 +573,13 @@
         sq = jnp.sum(projected * projected, axis=1, keepdims=True)
         return jnp.broadcast_to(sq, (r.stop - r.start, 128))
 
-    spread(last, 2, outside)
+    spread(last, 2, outside & (z > 0))
     landed(arrived.at[last, pl.ds(0, n_phase - 1), pl.ds(0, n_seq - 1)], all_recv.at[1])
     sq_top = complete(0)
     landed(arrived.at[last, pl.ds(0, n_phase - 1), pl.ds(0, 1)], all_recv.at[2])
+    rows_in(last, 2, z == 0)
     sq_all = jnp.concatenate([sq_top, complete(1)], axis=0)
-    sqbuf[p] = sq_all.T[0:8, :]
+    sqbuf[p] = sq_all.T[0:1, :]
     for other in partners:
         send(sqbuf.at[p], sqbuf.at[p], sq_send, sq_recv, {"phase": other})
     landed(sqbuf.at[pl.ds(0, n_phase - 1)], sq_recv)
@@ -578,8 +597,11 @@
     for dist in range(1, reach + 1):
         sent(halo.at[dist - 1, 0], h_send.at[dist - 1], (z >= dist - 1) & has_right)
         sent(halo.at[dist - 1, pl.ds(0, 3)], g_send.at[dist - 1], z >= dist)
-    sent(outrows.at[:, pl.ds(0, n_seq - 1)], row_send)
-    sent(arrived.at[:, pl.ds(0, n_phase - 1)], all_send)
+    sent(outrows.at[:, pl.ds(0, n_seq - 1)], row_send, inner)
+    sent(outrows.at[:, pl.ds(0, n_seq)], row_send, final)
+    sent(arrived.at[pl.ds(0, last), pl.ds(0, n_phase - 1)], all_send.at[0])
+    sent(arrived.at[last, pl.ds(0, n_phase - 1), pl.ds(0, n_seq - 1)], all_send.at[1])
+    sent(arrived.at[last, pl.ds(0, n_phase - 1), pl.ds(0, 1)], all_send.at[2], z > 0)
     sent(sqbuf.at[pl.ds(0, n_phase - 1)], sq_send)
 
 
@@ -633,7 +655,7 @@
             pltpu.VMEM((heads, n_phase, n_seq, slot, HD), bf),
             pltpu.VMEM((n_phase, n_seq * slot, cols), f32),
             pltpu.VMEM((reach + 1, tok, 3 * HD), f32),
-            pltpu.VMEM((n_phase, 8, n_seq * slot), f32),
+            pltpu.VMEM((n_phase, 1, n_seq * slot), f32),
             dma((7,)),
             dma(()),
             dma((heads, n_seq - 1)),
@@ -649,7 +671,7 @@
             dma((reach, 3)),
             dma(()),
             dma((heads, 3)),
-            dma(()),
+            dma((3,)),
             dma((3,)),
             dma(()),
             dma(()),

time: 67.8 us -> 66.9 us (0.987); the launches traced: 67.7 us -> 65.5 us
  Pallas kernels: 66.9 us -> 64.7 us
    pallas_call x1, Pallas kernels: 66 us -> 63.8 us  [fused(): pl.pallas_call(functools.partial(fused_kernel, (n_seq, n_phase, reach, sl...]
where the time goes in v6:
time: 66.9 us; the launch traced here: 65.5 us
  Pallas kernels  64.7 us (97%)
  between operations  0.8 us (1%)
    pallas_call x1, Pallas kernels, fused(): pl.pallas_call(functools.partial(fused_kernel, (n_seq, n_phase, reach, sl...  63.8 us

profile of v6, /device:TPU:0, one launch (start us, length us, event | category | flops | bytes accessed | tf_op | source)
XLA Modules:
  0.0 65.5 jit_solution(13125224987175938658)
XLA Ops:
  0.6 63.8 %shard_map.86 = (bf16[512,384]{1,0:T(8,128)(2,1)S(1)}, bf16[256,768]{1,0:T(8,128)(2,1)S(1)}) custom-call(bf16[512,1536]{1,0:T(8,128)(2,1)} %x_ref.1, f32[1536]{0:T(1024)} %gain_ref.1, bf16[3,384,384]{2,1,0:T(8,128)(2,1)} %bitcast.3, bf16[384,3072]{1,0:T(8,128)(2,1)} %up_ref.1, f32[768]{0:T(1024)} %og_ref.1, s32[1,128]{1,0:T(1,128)} %bitcast.4, s32[1,128]{1,0:T(1,128)} %bitcast.5), custom_call_target="tpu_custom_call" | custom-call | tf_op jit(solution)/shard_map/pallas_call | solution.py:632
  64.5 0.9 %shard_map.87 = (bf16[512,384]{1,0:T(8,128)(2,1)}, bf16[256,768]{1,0:T(8,128)(2,1)}) custom-call(bf16[512,384]{1,0:T(8,128)(2,1)S(1)} %get-tuple-element.4.a_ref, bf16[256,768]{1,0:T(8,128)(2,1)S(1)} %get-tuple-element.5.b_ref), custom_call_target="tpu_custom_call" | custom-call | tf_op jit(solution)/shard_map/pallas_call | solution.py:692

commit v7 on v6

--- a/solution.py
+++ b/solution.py
@@ -502,8 +502,8 @@
     for h in range(1, last):
         project(h, reach)
         close(h)
+    release(final)
     relay(last, 2, RIGHTWARD, final)
-    release(final)
     for t in range(3, n_seq):
         relay(last, t, RIGHTWARD, c == 1)
     for h in range(last):
@@ -517,14 +517,14 @@
     finish(last, True, final)
     for dist in range(reach + 1):
         project_late(dist, final)
+    for h in range(1, last):
+        spread(h, 1, final)
     for h in range(last):
         spread(h, 1, z == outer)
     project(last, reach, inner)
     close(last)
     spread(last, 1, z == outer)
     spread(last, 2, final)
-    for h in range(1, last):
-        spread(h, 1, final)
     for h in range(heads):
         spread(h, 0, final)
     landed(upbuf.at[0, up_half], up_recv.at[1])

time: 66.9 us -> 67 us (level)
  the two profiles are of different devices: /device:TPU:0 before, /device:TPU:24 now
where the time goes in v7:
time: 67 us; the launch traced here: 66.8 us
  Pallas kernels  66 us (99%)
  between operations  0.8 us (1%)
    pallas_call x1, Pallas kernels, fused(): pl.pallas_call(functools.partial(fused_kernel, (n_seq, n_phase, reach, sl...  65.1 us

profile of v7, /device:TPU:24, one launch (start us, length us, event | category | flops | bytes accessed | tf_op | source)
XLA Modules:
  0.0 66.8 jit_solution(5447066888627717162)
XLA Ops:
  0.6 65.1 %shard_map.86 = (bf16[512,384]{1,0:T(8,128)(2,1)S(1)}, bf16[256,768]{1,0:T(8,128)(2,1)S(1)}) custom-call(bf16[512,1536]{1,0:T(8,128)(2,1)} %x_ref.1, f32[1536]{0:T(1024)} %gain_ref.1, bf16[3,384,384]{2,1,0:T(8,128)(2,1)} %bitcast.3, bf16[384,3072]{1,0:T(8,128)(2,1)} %up_ref.1, f32[768]{0:T(1024)} %og_ref.1, s32[1,128]{1,0:T(1,128)} %bitcast.4, s32[1,128]{1,0:T(1,128)} %bitcast.5), custom_call_target="tpu_custom_call" | custom-call | tf_op jit(solution)/shard_map/pallas_call | solution.py:632
  65.8 0.9 %shard_map.87 = (bf16[512,384]{1,0:T(8,128)(2,1)}, bf16[256,768]{1,0:T(8,128)(2,1)}) custom-call(bf16[512,384]{1,0:T(8,128)(2,1)S(1)} %get-tuple-element.4.a_ref, bf16[256,768]{1,0:T(8,128)(2,1)S(1)} %get-tuple-element.5.b_ref), custom_call_target="tpu_custom_call" | custom-call | tf_op jit(solution)/shard_map/pallas_call | solution.py:692

commit v8 on v7

--- a/solution.py
+++ b/solution.py
@@ -395,7 +395,7 @@
                 pl.semaphore_signal(go, inc=1, device_id={"seq": far}, device_id_type=MESH)
 
     def rows_out(h, held):
-        for k in range(1, n_seq):
+        for k in reversed(range(1, n_seq)) if held else range(1, n_seq):
             other = lax.rem(z + k, n_seq)
             wait = (z < outer) & (other >= outer)
             send(

time: 67 us -> 66.6 us (level)
  the two profiles are of different devices: /device:TPU:24 before, /device:TPU:0 now
where the time goes in v8:
time: 66.6 us; the launch traced here: 65.6 us
  Pallas kernels  64.8 us (97%)
  between operations  0.8 us (1%)
    pallas_call x1, Pallas kernels, fused(): pl.pallas_call(functools.partial(fused_kernel, (n_seq, n_phase, reach, sl...  63.9 us

profile of v8, /device:TPU:0, one launch (start us, length us, event | category | flops | bytes accessed | tf_op | source)
XLA Modules:
  0.0 65.6 jit_solution(9622015714360335452)
XLA Ops:
  0.6 63.9 %shard_map.86 = (bf16[512,384]{1,0:T(8,128)(2,1)S(1)}, bf16[256,768]{1,0:T(8,128)(2,1)S(1)}) custom-call(bf16[512,1536]{1,0:T(8,128)(2,1)} %x_ref.1, f32[1536]{0:T(1024)} %gain_ref.1, bf16[3,384,384]{2,1,0:T(8,128)(2,1)} %bitcast.3, bf16[384,3072]{1,0:T(8,128)(2,1)} %up_ref.1, f32[768]{0:T(1024)} %og_ref.1, s32[1,128]{1,0:T(1,128)} %bitcast.4, s32[1,128]{1,0:T(1,128)} %bitcast.5), custom_call_target="tpu_custom_call" | custom-call | tf_op jit(solution)/shard_map/pallas_call | solution.py:632
  64.5 0.9 %shard_map.87 = (bf16[512,384]{1,0:T(8,128)(2,1)}, bf16[256,768]{1,0:T(8,128)(2,1)}) custom-call(bf16[512,384]{1,0:T(8,128)(2,1)S(1)} %get-tuple-element.4.a_ref, bf16[256,768]{1,0:T(8,128)(2,1)S(1)} %get-tuple-element.5.b_ref), custom_call_target="tpu_custom_call" | custom-call | tf_op jit(solution)/shard_map/pallas_call | solution.py:692
